TPU v7x, 32 devices: a whole 2x2x4 slice. The times are simulated.
32 devices in a mesh: ctx: 4 (over z), dp: 2 (over x), expert: 4 (over y, core).
Axes of the slice: x: 2, y: 2, z: 4, core: 2. Of those that a mesh axis runs over, the one named last changes fastest.
Arguments:
- tokens: bfloat16 [8, 1024, 2048], P(('dp', 'expert'), 'ctx'), may hold values from -6 to 6
- routes: int32 [8, 1024, 8], P(('dp', 'expert'), 'ctx'), may hold values from 0 to 15, all different within a row; in each aligned block of 256 rows (0 to 255, 256 to 511, ..., all dimensions but the last counted through in order) at most 176 rows name the same one
- w_query: bfloat16 [2048, 2048], replicated, may hold values from -0.125 to 0.125
- w_key: bfloat16 [2048, 2048], replicated, may hold values from -0.125 to 0.125
- w_value: bfloat16 [2048, 2048], replicated, may hold values from -0.125 to 0.125
- w_out: bfloat16 [2048, 2048], replicated, may hold values from -3 to 3
- attn_gain: float32 [2048], replicated, may hold values from 0.5 to 1.5
- query_gain: float32 [2048], replicated, may hold values from 0.5 to 1.5
- key_gain: float32 [2048], replicated, may hold values from 0.5 to 1.5
- mlp_gain: float32 [2048], replicated, may hold values from 0.5 to 1.5
- router: bfloat16 [2048, 16], replicated, may hold values from -0.125 to 0.125
- w_gate: bfloat16 [16, 2048, 1024], P('expert'), may hold values from -0.125 to 0.125
- w_up: bfloat16 [16, 2048, 1024], P('expert'), may hold values from -0.125 to 0.125
- w_down: bfloat16 [16, 1024, 2048], P('expert'), may hold values from -1.5 to 1.5
- cotangent: bfloat16 [8, 1024, 2048], P(('dp', 'expert'), 'ctx'), may hold values from -6 to 6
Outputs:
- mixed: bfloat16 [8, 1024, 2048], P(('dp', 'expert'), 'ctx')
- input_grad: float32 [8, 1024, 2048], P(('dp', 'expert'), 'ctx')
- grad_query: float32 [2048, 2048], P(('ctx', 'dp', 'expert'))
- grad_key: float32 [2048, 2048], P(('ctx', 'dp', 'expert'))
- grad_value: float32 [2048, 2048], P(('ctx', 'dp', 'expert'))
- grad_out: float32 [2048, 2048], P(('ctx', 'dp', 'expert'))
- grad_attn_gain: float32 [2048], P(('ctx', 'dp', 'expert'))
- grad_query_gain: float32 [2048], P(('ctx', 'dp', 'expert'))
- grad_key_gain: float32 [2048], P(('ctx', 'dp', 'expert'))
- grad_mlp_gain: float32 [2048], P(('ctx', 'dp', 'expert'))
- grad_router: float32 [2048, 16], P(('ctx', 'dp', 'expert'))
- grad_gate: float32 [16, 2048, 1024], P('expert', ('ctx', 'dp'))
- grad_up: float32 [16, 2048, 1024], P('expert', ('ctx', 'dp'))
- grad_down: float32 [16, 1024, 2048], P('expert', ('ctx', 'dp'))
Inputs may be any that keep to these rules, and one draw needn't show every extreme that they name: `routes`: each row names 8 different experts. Within each device's aligned block of 256 tokens no expert is named by more than 176 tokens, and some block reaches that bound.
All inputs are finite; a program needn't handle non-finite values.
Results may differ from a plain program's by a relative error of at most 0.03.
Values may be sent and summed in bfloat16 or wider, within the bound.
No kernel may reach another device: no remote copies, remote signals or barrier semaphores. Data moves between devices by JAX's collectives and lax.ppermute only.
A program may use at most 448 MiB of HBM per device.

v0:
```python
import functools

import jax
import jax.numpy as jnp
from jax import lax
from jax.experimental import pallas as pl
from jax.experimental.pallas import tpu as pltpu
from jax.sharding import PartitionSpec as P


HEADS = 16
HEAD_DIM = 128


EPSILON = 1e-05
FLOAT = jnp.float32
BRAIN = jnp.bfloat16
CTX = "ctx"
DP = "dp"
EXPERT = "expert"
OWN, FAR, NEAR, BOTH, GATES, UP_BOTH, BACK, STAGE = range(8)
NEAR_SUM, FAR_SUM, MADE, RING, HALF = range(8, 13)


def norm_inverse(values):
    return lax.rsqrt(jnp.mean(values * values, axis=-1, keepdims=True) + EPSILON)


def norm_backward(values, inverse, gain, upstream):
    weighted = upstream * gain
    gain_grad = jnp.sum(upstream * values * inverse, axis=0)
    value_grad = inverse * weighted - values * inverse * inverse * inverse * jnp.mean(
        weighted * values, axis=-1, keepdims=True
    )
    return (value_grad, gain_grad)


def rope_tables(positions):
    halfway = HEAD_DIM // 2
    frequency = 10000.0 ** (-jnp.arange(halfway, dtype=FLOAT) * 2.0 / HEAD_DIM)
    angles = positions.astype(FLOAT)[:, None] * frequency[None, :]
    angles = jnp.concatenate([angles, angles], axis=1)
    return (jnp.cos(angles), jnp.sin(angles))


def rotated(heads_rows, cosine, sine_table):
    halfway = HEAD_DIM // 2
    turned = jnp.concatenate([-heads_rows[..., halfway:], heads_rows[..., :halfway]], axis=-1)
    return heads_rows * cosine[:, None, :] + turned * sine_table[:, None, :]


def rotated_back(grads, cosine, sine_table):
    halfway = HEAD_DIM // 2
    sined = grads * sine_table[:, None, :]
    return grads * cosine[:, None, :] + jnp.concatenate(
        [sined[..., halfway:], -sined[..., :halfway]], axis=-1
    )


def outer_sum(left, right):
    return lax.dot_general(left, right, (((0,), (0,)), ((), ())), preferred_element_type=FLOAT)


def times_transpose(left, right):
    return lax.dot_general(left, right, (((1,), (1,)), ((), ())), preferred_element_type=FLOAT)


def times(left, right):
    return jnp.dot(left, right, preferred_element_type=FLOAT)


def plane_shards(
    tokens,
    routes,
    w_query,
    w_key,
    w_value,
    w_out,
    attn_gain,
    query_gain,
    key_gain,
    mlp_gain,
    router,
    w_gate,
    w_up,
    w_down,
    cotangent,
):
    inputs = tokens[0].astype(FLOAT)
    rows, width = inputs.shape
    ctx_count = lax.axis_size(CTX)
    dp_count = lax.axis_size(DP)
    expert_devices = lax.axis_size(EXPERT)
    plane = (DP, EXPERT)
    plane_count = dp_count * expert_devices
    everything = (CTX, DP, EXPERT)
    local_experts = w_gate.shape[0]
    experts_all = local_experts * expert_devices
    own_experts = local_experts // dp_count
    length = rows * ctx_count
    heads = HEADS // ctx_count
    columns = heads * HEAD_DIM
    score_scale = HEAD_DIM ** (-0.5)
    ctx_at = lax.axis_index(CTX)
    dp_at = lax.axis_index(DP)
    expert_at = lax.axis_index(EXPERT)
    first_column = ctx_at * columns

    attn_inverse = norm_inverse(inputs)
    attn_in = (inputs * attn_inverse * attn_gain).astype(BRAIN)
    all_in = lax.all_gather(attn_in, CTX, axis=0, tiled=True)
    upstream_low = cotangent[0]
    upstream = upstream_low.astype(FLOAT)
    all_upstream = lax.all_gather(upstream_low, plane, axis=0, tiled=True)

    qkv_weights = jnp.concatenate(
        [
            lax.dynamic_slice_in_dim(weights, first_column, columns, axis=1)
            for weights in (w_query, w_key, w_value)
        ],
        axis=1,
    )
    out_weights = lax.dynamic_slice_in_dim(w_out, first_column, columns, axis=0)
    query_gain_own = lax.dynamic_slice_in_dim(query_gain, first_column, columns, axis=0)
    key_gain_own = lax.dynamic_slice_in_dim(key_gain, first_column, columns, axis=0)
    inverses = jnp.concatenate(
        [norm_inverse(times(attn_in, w_query)), norm_inverse(times(attn_in, w_key))], axis=1
    )
    all_inverses = lax.all_gather(inverses, CTX, axis=0, tiled=True)
    query_inverse = all_inverses[:, 0:1]
    key_inverse = all_inverses[:, 1:2]
    cosine, sine_table = rope_tables(jnp.arange(length, dtype=jnp.int32))

    gate_weights, up_weights, down_weights = [
        lax.dynamic_slice_in_dim(weights, dp_at * own_experts, own_experts, axis=0)
        for weights in (w_gate, w_up, w_down)
    ]
    down_back = jnp.einsum(
        "td,efd->etf", all_upstream, down_weights, preferred_element_type=FLOAT
    )

    qkv_lin = times(all_in, qkv_weights)
    query_lin = qkv_lin[:, :columns]
    key_lin = qkv_lin[:, columns : 2 * columns]
    value_heads = qkv_lin[:, 2 * columns :].astype(BRAIN).reshape(length, heads, HEAD_DIM)
    query_heads = rotated(
        (query_lin * query_inverse * query_gain_own).reshape(length, heads, HEAD_DIM),
        cosine,
        sine_table,
    ).astype(BRAIN)
    key_heads = rotated(
        (key_lin * key_inverse * key_gain_own).reshape(length, heads, HEAD_DIM), cosine, sine_table
    ).astype(BRAIN)
    positions = jnp.arange(length, dtype=jnp.int32)
    visible = (positions[None, :] <= positions[:, None])[None]
    scores = (
        jnp.einsum("qhd,khd->hqk", query_heads, key_heads, preferred_element_type=FLOAT)
        * score_scale
    )
    scores = jnp.where(visible, scores, -1e30)
    probs = jax.nn.softmax(scores, axis=-1)
    probs_low = probs.astype(BRAIN)
    attn_wide = jnp.einsum("hqk,khd->qhd", probs_low, value_heads, preferred_element_type=FLOAT)
    attn_own = attn_wide.astype(BRAIN).reshape(length, columns)
    attn_rows = lax.all_to_all(attn_own, CTX, split_axis=0, concat_axis=1, tiled=True)
    hidden = inputs + times(attn_rows, w_out)
    mlp_inverse = norm_inverse(hidden)
    expert_in = (hidden * mlp_inverse * mlp_gain).astype(BRAIN)
    all_expert_in = lax.all_gather(expert_in, plane, axis=0, tiled=True)
    logits = times(expert_in, router)
    gate_probs = jax.nn.softmax(logits, axis=-1)
    chosen = jnp.any(
        routes[0][:, :, None] == jnp.arange(experts_all, dtype=jnp.int32)[None, None, :], axis=1
    )
    gates = jnp.where(chosen, gate_probs, 0.0)
    all_gates = lax.all_gather(gates, plane, axis=0, tiled=True)
    first_expert = expert_at * local_experts + dp_at * own_experts
    own_gates = lax.dynamic_slice_in_dim(all_gates, first_expert, own_experts, axis=1).T[:, :, None]

    gate_pre = jnp.einsum(
        "td,edf->etf", all_expert_in, gate_weights, preferred_element_type=FLOAT
    )
    up_pre = jnp.einsum("td,edf->etf", all_expert_in, up_weights, preferred_element_type=FLOAT)
    sigmoid_gate = jax.nn.sigmoid(gate_pre)
    silu_gate = gate_pre * sigmoid_gate
    activated = silu_gate * up_pre
    weighted = (own_gates * activated).astype(BRAIN)
    own_gate_grads = jnp.sum(down_back * activated, axis=-1).T
    act_grad = own_gates * down_back
    up_grad = (act_grad * silu_gate).astype(BRAIN)
    gate_grad = (act_grad * up_pre * sigmoid_gate * (1.0 + gate_pre * (1.0 - sigmoid_gate))).astype(
        BRAIN
    )
    input_rows = (
        jnp.einsum("etf,edf->td", gate_grad, gate_weights, preferred_element_type=FLOAT)
        + jnp.einsum("etf,edf->td", up_grad, up_weights, preferred_element_type=FLOAT)
    ).astype(BRAIN)
    expert_in_grad = lax.psum_scatter(input_rows, plane, scatter_dimension=0, tiled=True).astype(
        FLOAT
    )
    produced = jnp.einsum(
        "etf,efd->td", weighted, down_weights, preferred_element_type=FLOAT
    ).astype(BRAIN)
    mixed = hidden + lax.psum_scatter(produced, plane, scatter_dimension=0, tiled=True).astype(
        FLOAT
    )
    gate_grads = lax.all_to_all(
        own_gate_grads.reshape(plane_count, rows, own_experts),
        plane,
        split_axis=0,
        concat_axis=0,
        tiled=True,
    )
    gate_grads = (
        gate_grads.reshape(dp_count, expert_devices, rows, own_experts)
        .transpose(2, 1, 0, 3)
        .reshape(rows, experts_all)
    )

    def spread(partial):
        summed = lax.psum_scatter(partial.astype(BRAIN), CTX, scatter_dimension=1, tiled=True)
        return lax.all_to_all(summed, DP, split_axis=1, concat_axis=0, tiled=True).astype(FLOAT)

    down_weight_grad = spread(
        jnp.einsum("etf,td->efd", weighted, all_upstream, preferred_element_type=FLOAT)
    )
    gate_weight_grad = spread(
        jnp.einsum("td,etf->edf", all_expert_in, gate_grad, preferred_element_type=FLOAT)
    )
    up_weight_grad = spread(
        jnp.einsum("td,etf->edf", all_expert_in, up_grad, preferred_element_type=FLOAT)
    )

    prob_grads = jnp.where(chosen, gate_grads, 0.0)
    logit_grads = (
        gate_probs * (prob_grads - jnp.sum(prob_grads * gate_probs, axis=-1, keepdims=True))
    ).astype(BRAIN)
    router_grad = outer_sum(expert_in, logit_grads)
    expert_in_grad = expert_in_grad + times_transpose(logit_grads, router)
    hidden_part, mlp_gain_grad = norm_backward(hidden, mlp_inverse, mlp_gain, expert_in_grad)
    hidden_grad = upstream + hidden_part
    hidden_low = hidden_grad.astype(BRAIN)
    all_hidden_low = lax.all_gather(hidden_low, CTX, axis=0, tiled=True)
    attn_grad = times_transpose(all_hidden_low, out_weights).astype(BRAIN)
    attn_grad_heads = attn_grad.reshape(length, heads, HEAD_DIM)
    out_weight_grad = lax.psum_scatter(
        outer_sum(attn_own, all_hidden_low).astype(BRAIN), plane, scatter_dimension=0, tiled=True
    ).astype(FLOAT)
    row_delta = jnp.sum(attn_wide * attn_grad_heads.astype(FLOAT), axis=-1).T
    prob_grad = jnp.einsum(
        "qhd,khd->hqk", attn_grad_heads, value_heads, preferred_element_type=FLOAT
    )
    score_grad = (probs * (prob_grad - row_delta[..., None])).astype(BRAIN)
    query_grad = (
        jnp.einsum("hqk,khd->qhd", score_grad, key_heads, preferred_element_type=FLOAT)
        * score_scale
    )
    key_grad = (
        jnp.einsum("hqk,qhd->khd", score_grad, query_heads, preferred_element_type=FLOAT)
        * score_scale
    )
    value_low = (
        jnp.einsum("hqk,qhd->khd", probs_low, attn_grad_heads, preferred_element_type=FLOAT)
        .astype(BRAIN)
        .reshape(length, columns)
    )
    query_rot_grad = rotated_back(query_grad, cosine, sine_table).reshape(length, columns)
    key_rot_grad = rotated_back(key_grad, cosine, sine_table).reshape(length, columns)
    query_weighted = query_rot_grad * query_gain_own
    key_weighted = key_rot_grad * key_gain_own
    dots = lax.psum(
        jnp.stack(
            [jnp.sum(query_weighted * query_lin, axis=-1), jnp.sum(key_weighted * key_lin, axis=-1)]
        ),
        CTX,
    ) * (1.0 / width)
    query_gain_grad = jnp.sum(query_rot_grad * query_lin * query_inverse, axis=0)
    key_gain_grad = jnp.sum(key_rot_grad * key_lin * key_inverse, axis=0)
    query_low = (
        query_inverse * query_weighted
        - query_lin * (query_inverse * query_inverse * query_inverse * dots[0][:, None])
    ).astype(BRAIN)
    key_low = (
        key_inverse * key_weighted
        - key_lin * (key_inverse * key_inverse * key_inverse * dots[1][:, None])
    ).astype(BRAIN)
    qkv_low = jnp.concatenate([query_low, key_low, value_low], axis=1)
    attn_in_grad = lax.psum_scatter(
        times_transpose(qkv_low, qkv_weights).astype(BRAIN), CTX, scatter_dimension=0, tiled=True
    ).astype(FLOAT)
    qkv_weight_grad = outer_sum(all_in, qkv_low).astype(BRAIN)
    qkv_weight_grad = lax.psum_scatter(
        qkv_weight_grad.reshape(ctx_count, width // ctx_count, 3 * columns),
        plane,
        scatter_dimension=1,
        tiled=True,
    )
    qkv_weight_grad = lax.all_to_all(
        qkv_weight_grad, CTX, split_axis=0, concat_axis=0, tiled=True
    )
    out_rows = qkv_weight_grad.shape[1]
    qkv_weight_grad = (
        qkv_weight_grad.reshape(ctx_count, out_rows, 3, columns)
        .transpose(2, 1, 0, 3)
        .reshape(3, out_rows, width)
        .astype(FLOAT)
    )
    input_part, attn_gain_grad = norm_backward(inputs, attn_inverse, attn_gain, attn_in_grad)
    input_grad = hidden_grad + input_part

    empty = jnp.zeros((width,), FLOAT)
    small = jnp.concatenate(
        [
            jnp.stack(
                [
                    attn_gain_grad,
                    lax.dynamic_update_slice_in_dim(empty, query_gain_grad, first_column, axis=0),
                    lax.dynamic_update_slice_in_dim(empty, key_gain_grad, first_column, axis=0),
                    mlp_gain_grad,
                ],
                axis=1,
            ),
            router_grad,
        ],
        axis=1,
    )
    small = lax.psum_scatter(small, everything, scatter_dimension=0, tiled=True)
    return (
        mixed.astype(BRAIN)[None],
        input_grad[None],
        qkv_weight_grad[0],
        qkv_weight_grad[1],
        qkv_weight_grad[2],
        out_weight_grad,
        small[:, 0],
        small[:, 1],
        small[:, 2],
        small[:, 3],
        small[:, 4:],
        gate_weight_grad,
        up_weight_grad,
        down_weight_grad,
    )


def meet(*values):
    return lax.optimization_barrier(values)


def stage_body(
    slot,
    count,
    units,
    place,
    own,
    far,
    near,
    both,
    back,
    gates,
    weights,
    weights_back,
    *rest,
):
    row_outs = rest[-12:-8]
    gate_grads_out, rows_out, grads_out, weighted_out = rest[-8:-4]
    held, grads, in_sems, out_sem = rest[-4:]
    step = pl.program_id(0)
    rows = own.shape[0]
    whole = rows_out.at[pl.ds(slot * 4 * rows, 4 * rows), :]

    @pl.when(step == 0)
    def _():
        copies = [
            pltpu.make_async_copy(block, held.at[pl.ds(at * rows, rows), :], in_sems.at[at])
            for at, block in enumerate((own, far, near, both))
        ]
        for copy in copies:
            copy.start()
        gate_grads_out[...] = jnp.zeros_like(gate_grads_out)
        for copy in copies:
            copy.wait()
        pltpu.make_async_copy(held, whole, out_sem).start()

    @pl.when(step < count)
    def _():
        lane = lax.broadcasted_iota(jnp.int32, (rows, gates.shape[1]), 1)
        wanted = lane == place[0] + step

        def one(at, carry):
            part = pl.ds(pl.multiple_of(at * rows, rows), rows)
            pre = jnp.dot(held[part, :], weights[0], preferred_element_type=FLOAT)
            gate_pre, up_pre = pre[:, :units], pre[:, units:]
            down_back = back[part, :].astype(FLOAT)
            gate = jnp.sum(
                jnp.where(wanted, gates[part, :].astype(FLOAT), 0.0), axis=1, keepdims=True
            )
            sigmoid = jax.nn.sigmoid(gate_pre)
            silu = gate_pre * sigmoid
            activated = silu * up_pre
            weighted_out[part, :] = (gate * activated).astype(BRAIN)
            gate_grad = jnp.sum(down_back * activated, axis=1, keepdims=True)
            gate_grads_out[part, :] += jnp.where(wanted, gate_grad, 0.0)
            act_grad = gate * down_back
            gate_side = (
                act_grad * up_pre * sigmoid * (1.0 + gate_pre * (1.0 - sigmoid))
            ).astype(BRAIN)
            up_side = (act_grad * silu).astype(BRAIN)
            grads_out[part, :units] = gate_side
            grads_out[part, units:] = up_side
            first = pl.multiple_of(step * 2 * units, 2 * units)
            grads[part, pl.ds(first, units)] = gate_side
            grads[part, pl.ds(first + units, units)] = up_side
            return carry

        lax.fori_loop(0, 4, one, 0, unroll=4)

    @pl.when(step >= count)
    def _():
        for at in range(4):
            row_outs[at][...] = jnp.dot(
                grads[at * rows : (at + 1) * rows, :],
                weights_back[...],
                preferred_element_type=FLOAT,
            ).astype(BRAIN)

    @pl.when(step == pl.num_programs(0) - 1)
    def _():
        pltpu.make_async_copy(held, whole, out_sem).wait()


def expert_stage(slot, place, blocks, down_back, gates, weights, weights_back, buffers):
    rows, width = blocks[0].shape
    count, _, both_units = weights.shape
    units = both_units // 2
    stage_rows = 4 * rows
    tiles = 4
    tile = width // tiles
    all_rows = down_back.shape[0]
    anywhere = pl.BlockSpec(memory_space=pl.ANY)

    def first_part(step):
        return jnp.minimum(step, count - 1)

    def second_part(step):
        return jnp.maximum(step - count, 0)

    whole_specs = [
        anywhere,
        pl.BlockSpec((stage_rows, both_units), lambda i, p: (slot, first_part(i))),
        pl.BlockSpec((stage_rows, units), lambda i, p: (slot, first_part(i))),
    ]
    whole_shapes = [
        jax.ShapeDtypeStruct((all_rows, width), BRAIN),
        jax.ShapeDtypeStruct((all_rows, count * both_units), BRAIN),
        jax.ShapeDtypeStruct((all_rows, count * units), BRAIN),
    ]
    previous = () if buffers is None else tuple(buffers)
    return pl.pallas_call(
        functools.partial(stage_body, slot, count, units),
        grid_spec=pltpu.PrefetchScalarGridSpec(
            num_scalar_prefetch=1,
            grid=(count + tiles,),
            in_specs=[anywhere] * 4
            + [
                pl.BlockSpec((stage_rows, units), lambda i, p: (slot, first_part(i))),
                pl.BlockSpec((stage_rows, gates.shape[1]), lambda i, p: (0, 0)),
                pl.BlockSpec((1, width, both_units), lambda i, p: (first_part(i), 0, 0)),
                pl.BlockSpec((count * both_units, tile), lambda i, p: (0, second_part(i))),
            ]
            + [anywhere] * len(previous),
            out_specs=[pl.BlockSpec((rows, tile), lambda i, p: (0, second_part(i)))] * 4
            + [pl.BlockSpec((stage_rows, gates.shape[1]), lambda i, p: (0, 0))]
            + whole_specs,
            scratch_shapes=[
                pltpu.VMEM((stage_rows, width), BRAIN),
                pltpu.VMEM((stage_rows, count * both_units), BRAIN),
                pltpu.SemaphoreType.DMA((4,)),
                pltpu.SemaphoreType.DMA,
            ],
        ),
        out_shape=[jax.ShapeDtypeStruct((rows, width), BRAIN)] * 4
        + [jax.ShapeDtypeStruct((stage_rows, gates.shape[1]), FLOAT)]
        + whole_shapes,
        input_output_aliases={9 + at: 5 + at for at in range(len(previous))},
        compiler_params=pltpu.CompilerParams(dimension_semantics=("arbitrary",)),
        cost_estimate=pl.CostEstimate(
            flops=4 * stage_rows * width * count * both_units,
            bytes_accessed=40 << 20,
            transcendentals=stage_rows * count * units,
        ),
        name="expert_stage",
    )(place, *blocks, down_back, gates, weights, weights_back, *previous)


def back_body(count, *refs):
    blocks = refs[: 4 * count]
    weights, rows_out, back_out, held, in_sems, out_sems = refs[4 * count :]
    step = pl.program_id(0)
    rows = blocks[0].shape[0]

    def incoming(slot):
        return [
            pltpu.make_async_copy(
                blocks[4 * slot + at],
                held.at[slot % 2, pl.ds(at * rows, rows), :],
                in_sems.at[slot % 2, at],
            )
            for at in range(4)
        ]

    def outgoing(slot):
        return pltpu.make_async_copy(
            held.at[slot % 2],
            rows_out.at[pl.ds(slot * 4 * rows, 4 * rows), :],
            out_sems.at[slot % 2],
        )

    for slot in range(count):

        @pl.when(step == slot)
        def _(slot=slot):
            if slot == 0:
                for copy in incoming(0):
                    copy.start()
            if slot > 0:
                outgoing(slot - 1).wait()
            if slot + 1 < count:
                for copy in incoming(slot + 1):
                    copy.start()
            for copy in incoming(slot):
                copy.wait()
            outgoing(slot).start()

    def one(at, carry):
        part = pl.ds(pl.multiple_of(at * rows, rows), rows)
        back_out[part, :] = jnp.dot(
            held[lax.rem(step, 2), part, :], weights[...], preferred_element_type=FLOAT
        ).astype(BRAIN)
        return carry

    lax.fori_loop(0, 4, one, 0)

    @pl.when(step == count - 1)
    def _():
        outgoing(count - 1).wait()


def gathered_back(blocks, weights):
    rows, width = blocks[0].shape
    count = len(blocks) // 4
    units = weights.shape[1]
    anywhere = pl.BlockSpec(memory_space=pl.ANY)
    return pl.pallas_call(
        functools.partial(back_body, count),
        grid=(count,),
        in_specs=[anywhere] * len(blocks) + [pl.BlockSpec((width, units), lambda i: (0, 0))],
        out_specs=[anywhere, pl.BlockSpec((4 * rows, units), lambda i: (i, 0))],
        scratch_shapes=[
            pltpu.VMEM((2, 4 * rows, width), BRAIN),
            pltpu.SemaphoreType.DMA((2, 4)),
            pltpu.SemaphoreType.DMA((2,)),
        ],
        out_shape=[
            jax.ShapeDtypeStruct((4 * rows * count, width), BRAIN),
            jax.ShapeDtypeStruct((4 * rows * count, units), BRAIN),
        ],
        compiler_params=pltpu.CompilerParams(dimension_semantics=("arbitrary",)),
        cost_estimate=pl.CostEstimate(
            flops=8 * rows * count * width * units,
            bytes_accessed=48 << 20,
            transcendentals=0,
        ),
        name="gathered_back",
    )(*blocks, weights)


def placed_body(pairs, units, places, *refs):
    parts, outs = refs[:-2], refs[-2:]
    slots = len(parts) // 2
    for half in (0, 1):
        for slot in range(slots):
            lanes = pl.ds(pl.multiple_of(places[slot] * units, units), units)
            part = parts[half * slots + slot]
            for pair in range(pairs):
                for side in (0, 1):
                    first = (2 * pair + side) * units
                    outs[side][half * pairs + pair, :, lanes] = part[
                        :, first : first + units
                    ].astype(FLOAT)


def placed_grads(places, parts, local_experts, units):
    rows = parts[0].shape[0]
    slots = len(parts) // 2
    shape = (local_experts, rows, slots * units)
    return pl.pallas_call(
        functools.partial(placed_body, local_experts // 2, units),
        in_specs=[pl.BlockSpec(memory_space=pltpu.SMEM)]
        + [pl.BlockSpec(memory_space=pltpu.VMEM)] * len(parts),
        out_specs=[pl.BlockSpec(memory_space=pltpu.VMEM)] * 2,
        out_shape=[jax.ShapeDtypeStruct(shape, FLOAT)] * 2,
        cost_estimate=pl.CostEstimate(
            flops=8 * rows * slots * units, bytes_accessed=12 << 20, transcendentals=0
        ),
        name="placed_grads",
    )(places, *parts)


def swap_over(values, axis, bit):
    count = lax.axis_size(axis)
    return lax.ppermute(values, axis, [(at, at ^ bit) for at in range(count)])


def shift_over(values, axis, steps):
    count = lax.axis_size(axis)
    return lax.ppermute(values, axis, [(at, (at + steps) % count) for at in range(count)])


def axis_bits(axis):
    count = lax.axis_size(axis)
    return [1 << at for at in reversed(range(count.bit_length() - 1))]


def line_shards(
    tokens,
    routes,
    w_query,
    w_key,
    w_value,
    w_out,
    attn_gain,
    query_gain,
    key_gain,
    mlp_gain,
    router,
    w_gate,
    w_up,
    w_down,
    cotangent,
):
    inputs = tokens[0].astype(FLOAT)
    rows, width = inputs.shape
    ctx_count = lax.axis_size(CTX)
    dp_count = lax.axis_size(DP)
    expert_devices = lax.axis_size(EXPERT)
    plane = (DP, EXPERT)
    device_count = ctx_count * dp_count * expert_devices
    local_experts, _, units_all = w_gate.shape
    experts_all = local_experts * expert_devices
    units = units_all // ctx_count
    hidden_units = local_experts * units
    length = rows * ctx_count
    heads = HEADS // ctx_count
    columns = heads * HEAD_DIM
    score_scale = HEAD_DIM ** (-0.5)
    ctx_at = lax.axis_index(CTX)
    dp_at = lax.axis_index(DP)
    expert_at = lax.axis_index(EXPERT)
    first_column = ctx_at * columns
    ring_places = [(ctx_at + ctx_count - slot) % ctx_count for slot in range(ctx_count)]

    attn_inverse = norm_inverse(inputs)
    attn_in = (inputs * attn_inverse * attn_gain).astype(BRAIN)
    all_in = lax.all_gather(attn_in, CTX, axis=0, tiled=True)
    inverses = jnp.concatenate(
        [norm_inverse(times(attn_in, w_query)), norm_inverse(times(attn_in, w_key))], axis=1
    )
    all_inverses = lax.all_gather(inverses, CTX, axis=0, tiled=True)
    query_inverse = all_inverses[:, 0:1]
    key_inverse = all_inverses[:, 1:2]

    qkv_weights = jnp.concatenate(
        [
            lax.dynamic_slice_in_dim(weights, first_column, columns, axis=1)
            for weights in (w_query, w_key, w_value)
        ],
        axis=1,
    )
    query_gain_own = lax.dynamic_slice_in_dim(query_gain, first_column, columns, axis=0)
    key_gain_own = lax.dynamic_slice_in_dim(key_gain, first_column, columns, axis=0)
    cosine, sine_table = rope_tables(jnp.arange(length, dtype=jnp.int32))
    gate_slice, up_slice = [
        lax.dynamic_slice_in_dim(weights, ctx_at * units, units, axis=2)
        for weights in (w_gate, w_up)
    ]
    gate_up_weights = jnp.concatenate([gate_slice, up_slice], axis=2)
    gate_up_back = gate_up_weights.transpose(0, 2, 1).reshape(2 * hidden_units, width)
    down_weights = lax.dynamic_slice_in_dim(w_down, ctx_at * units, units, axis=1).reshape(
        hidden_units, width
    )

    down_across = down_weights.T
    all_in, upstream_low, gate_up_weights, gate_up_back, down_weights, down_across, qkv_weights = (
        meet(
            all_in,
            cotangent[0],
            gate_up_weights,
            gate_up_back,
            down_weights,
            down_across,
            qkv_weights,
        )
    )
    upstream = upstream_low.astype(FLOAT)
    near, far = axis_bits(EXPERT)[::-1]
    up_own = [upstream_low]
    up_own.append(shift_over(up_own[0], CTX, 1))
    up_far = [swap_over(up_own[0], EXPERT, far)]

    qkv_lin = times(all_in, qkv_weights)
    query_lin = qkv_lin[:, :columns]
    key_lin = qkv_lin[:, columns : 2 * columns]
    value_heads = qkv_lin[:, 2 * columns :].astype(BRAIN).reshape(length, heads, HEAD_DIM)
    query_heads = rotated(
        (query_lin * query_inverse * query_gain_own).reshape(length, heads, HEAD_DIM),
        cosine,
        sine_table,
    ).astype(BRAIN)
    key_heads = rotated(
        (key_lin * key_inverse * key_gain_own).reshape(length, heads, HEAD_DIM), cosine, sine_table
    ).astype(BRAIN)
    query_heads, key_heads, up_own[1], up_far[0] = meet(
        query_heads, key_heads, up_own[1], up_far[0]
    )
    up_own.append(shift_over(up_own[1], CTX, 1))
    up_far.append(swap_over(up_own[1], EXPERT, far))
    up_near = [swap_over(up_own[0], EXPERT, near)]
    up_both = [swap_over(up_far[0], EXPERT, near)]
    positions = jnp.arange(length, dtype=jnp.int32)
    visible = (positions[None, :] <= positions[:, None])[None]
    scores = (
        jnp.einsum("qhd,khd->hqk", query_heads, key_heads, preferred_element_type=FLOAT)
        * score_scale
    )
    scores = jnp.where(visible, scores, -1e30)
    probs = jax.nn.softmax(scores, axis=-1)
    probs_low = probs.astype(BRAIN)
    attn_wide = jnp.einsum("hqk,khd->qhd", probs_low, value_heads, preferred_element_type=FLOAT)
    attn_own = attn_wide.astype(BRAIN).reshape(length, columns)
    attn_own, up_own, up_far, up_near, up_both = meet(attn_own, up_own, up_far, up_near, up_both)
    up_far.append(swap_over(up_own[2], EXPERT, far))
    up_near.append(swap_over(up_own[1], EXPERT, near))
    up_near.append(swap_over(up_own[2], EXPERT, near))
    up_both.append(swap_over(up_far[1], EXPERT, near))
    attn_rows = lax.all_to_all(attn_own, CTX, split_axis=0, concat_axis=1, tiled=True)
    attn_rows, up_own, up_far, up_near, up_both = meet(
        attn_rows, up_own, up_far, up_near, up_both
    )
    up_own.append(shift_over(up_own[2], CTX, 1))
    up_both.append(swap_over(up_far[2], EXPERT, near))
    up_far.append(swap_over(up_own[3], EXPERT, far))
    up_near.append(swap_over(up_own[3], EXPERT, near))
    hidden = inputs + times(attn_rows, w_out)
    mlp_inverse = norm_inverse(hidden)
    expert_in = (hidden * mlp_inverse * mlp_gain).astype(BRAIN)
    logits = times(expert_in, router)
    gate_probs = jax.nn.softmax(logits, axis=-1)
    chosen = jnp.any(
        routes[0][:, :, None] == jnp.arange(experts_all, dtype=jnp.int32)[None, None, :], axis=1
    )
    gates = jnp.where(chosen, gate_probs, 0.0).astype(BRAIN)

    def dp_parts(partial, outer, inner):
        halves = partial.reshape(outer, dp_count, inner, -1)
        return (
            lax.dynamic_index_in_dim(halves, dp_at, axis=1, keepdims=False),
            swap_over(
                lax.dynamic_index_in_dim(halves, 1 - dp_at, axis=1, keepdims=False), DP, 1
            ),
        )

    def ctx_parts(blocks):
        return [
            shift_over(
                lax.dynamic_index_in_dim(
                    blocks, (ctx_at + at) % ctx_count, axis=0, keepdims=False
                ),
                CTX,
                at,
            )
            if at
            else lax.dynamic_index_in_dim(blocks, ctx_at, axis=0, keepdims=False)
            for at in range(ctx_count)
        ]

    grad_rows = width // (ctx_count * dp_count)
    padded_gates = jnp.pad(gates, ((0, 0), (0, -experts_all % 128)))
    first_expert = expert_at * local_experts
    expert_place = jnp.full((1,), first_expert, jnp.int32)

    moved_own = [expert_in]
    moved_far, moved_near, moved_both = [], [], []
    gate_slots, stages, near_sums, far_sums, half_grads = [], [], [], [], []
    buffers = produced = sent = total = total_gate = None
    gate_half = padded_gates
    for tick in range(ctx_count + 5):
        slot = tick - 2
        fresh = {}
        if tick + 1 < ctx_count:
            fresh[OWN] = shift_over(moved_own[tick], CTX, 1)
        if tick < ctx_count:
            fresh[FAR] = swap_over(moved_own[tick], EXPERT, far)
            fresh[NEAR] = swap_over(moved_own[tick], EXPERT, near)
        if 0 <= tick - 1 < ctx_count:
            fresh[BOTH] = swap_over(moved_far[tick - 1], EXPERT, near)
        if tick == 0:
            fresh[GATES] = jnp.concatenate([gate_half, swap_over(gate_half, EXPERT, far)])
            fresh[UP_BOTH] = swap_over(up_far[3], EXPERT, near)
        if tick == 1:
            fresh[GATES] = jnp.concatenate([gate_half, swap_over(gate_half, EXPERT, near)])
            fresh[BACK] = gathered_back(
                [
                    kind[at]
                    for at in range(ctx_count)
                    for kind in (up_own, up_far, up_near, up_both)
                ],
                down_across,
            )
        if 2 <= tick < ctx_count + 1:
            fresh[GATES] = shift_over(gate_slots[-1], CTX, 1)
        if 0 <= slot < ctx_count:
            fresh[STAGE] = expert_stage(
                slot,
                expert_place,
                (moved_own[slot], moved_far[slot], moved_near[slot], moved_both[slot]),
                down_back,
                gate_slots[slot],
                gate_up_weights,
                gate_up_back,
                buffers,
            )
        if 0 <= slot - 1 < ctx_count:
            grads = stages[slot - 1]
            gate_part = grads[4].astype(BRAIN)
            fresh[NEAR_SUM] = (
                grads[0] + swap_over(grads[2], EXPERT, near),
                grads[1] + swap_over(grads[3], EXPERT, near),
                gate_part[: 2 * rows] + swap_over(gate_part[2 * rows :], EXPERT, near),
            )
        if 0 <= slot - 2 < ctx_count:
            pair = near_sums[slot - 2]
            fresh[FAR_SUM] = (
                pair[0] + swap_over(pair[1], EXPERT, far),
                pair[2][:rows] + swap_over(pair[2][rows:], EXPERT, far),
            )
        if tick == ctx_count + 2:
            total, total_gate = far_sums[1]
            all_rows, all_pre_grads, all_weighted = buffers
            fresh[MADE] = [
                [
                    times(
                        all_weighted[(4 * at + 2 * part) * rows :][: 2 * rows], down_weights
                    ).astype(BRAIN)
                    for part in (0, 1)
                ]
                for at in range(ctx_count)
            ]
        if tick >= ctx_count + 2:
            fresh[RING] = (shift_over(total, CTX, 1), shift_over(total_gate, CTX, 1))
        if tick == ctx_count + 3:
            fresh[MADE] = []
            for kept, given in produced:
                taken = swap_over(given, EXPERT, near)
                fresh[MADE].append((kept[:rows] + taken[:rows], kept[rows:] + taken[rows:]))
        if tick == ctx_count + 4:
            fresh[MADE] = [produced[1][0] + swap_over(produced[1][1], EXPERT, far), produced]
            first_parts = dp_parts(half_grads[0], ctx_count, grad_rows)
        if tick >= ctx_count + 3:
            half = tick - ctx_count - 3
            fresh[HALF] = outer_sum(
                all_rows, all_pre_grads[:, half * hidden_units :][:, :hidden_units]
            ).astype(BRAIN)
        fresh = meet(fresh)[0]
        if OWN in fresh:
            moved_own.append(fresh[OWN])
        if FAR in fresh:
            moved_far.append(fresh[FAR])
            moved_near.append(fresh[NEAR])
        if BOTH in fresh:
            moved_both.append(fresh[BOTH])
        if tick == 0:
            up_both.append(fresh[UP_BOTH])
            gate_half = fresh[GATES]
        elif GATES in fresh:
            gate_slots.append(fresh[GATES])
        if BACK in fresh:
            all_upstream, down_back = fresh[BACK]
        if STAGE in fresh:
            stages.append(fresh[STAGE][:5])
            buffers = fresh[STAGE][5:]
        if NEAR_SUM in fresh:
            near_sums.append(fresh[NEAR_SUM])
        if FAR_SUM in fresh:
            far_sums.append(fresh[FAR_SUM])
        if RING in fresh:
            following = far_sums[(tick - ctx_count) % ctx_count]
            total = fresh[RING][0] + following[0]
            total_gate = fresh[RING][1] + following[1]
        if MADE in fresh:
            produced = fresh[MADE]
        if HALF in fresh:
            half_grads.append(fresh[HALF])
    expert_in_grad = total.astype(FLOAT)
    gate_grads = total_gate[:, :experts_all].astype(FLOAT)
    produced_total, produced = produced

    prob_grads = jnp.where(chosen, gate_grads, 0.0)
    logit_grads = (
        gate_probs * (prob_grads - jnp.sum(prob_grads * gate_probs, axis=-1, keepdims=True))
    ).astype(BRAIN)
    router_grad = outer_sum(expert_in, logit_grads)
    expert_in_grad = expert_in_grad + times_transpose(logit_grads, router)
    hidden_part, mlp_gain_grad = norm_backward(hidden, mlp_inverse, mlp_gain, expert_in_grad)
    hidden_grad = upstream + hidden_part
    hidden_low = hidden_grad.astype(BRAIN)
    attn_grad_rows = times_transpose(hidden_low, w_out).astype(BRAIN)
    second_parts = dp_parts(half_grads[1], ctx_count, grad_rows)
    produced_two = produced[2][0] + swap_over(produced[2][1], EXPERT, far)
    produced_three = produced[3][0] + swap_over(produced[3][1], EXPERT, far)
    produced_total = shift_over(produced_total, CTX, 1)
    attn_grad_rows, first_parts = meet(attn_grad_rows, first_parts)
    attn_grad = lax.all_to_all(
        attn_grad_rows.reshape(rows, ctx_count, columns).transpose(1, 0, 2),
        CTX,
        split_axis=0,
        concat_axis=0,
        tiled=True,
    ).reshape(length, columns)
    first_half = ctx_parts(first_parts[0] + first_parts[1])
    down_half = outer_sum(all_weighted, all_upstream).astype(BRAIN)
    attn_grad, produced_two, produced_three, down_half, produced, hidden_low, produced_total = meet(
        attn_grad, produced_two, produced_three, down_half, produced, hidden_low, produced_total
    )
    attn_grad_heads = attn_grad.reshape(length, heads, HEAD_DIM)
    out_weight_grad = outer_sum(attn_rows, hidden_low).astype(BRAIN)
    out_weight_grad = lax.psum_scatter(
        out_weight_grad.reshape(ctx_count, width // ctx_count, width),
        plane,
        scatter_dimension=1,
        tiled=True,
    )
    produced_zero = produced[0][0] + swap_over(produced[0][1], EXPERT, far)
    produced_total = shift_over(produced_total + produced_two, CTX, 1)
    row_delta = jnp.sum(attn_wide * attn_grad_heads.astype(FLOAT), axis=-1).T
    prob_grad = jnp.einsum(
        "qhd,khd->hqk", attn_grad_heads, value_heads, preferred_element_type=FLOAT
    )
    score_grad = (probs * (prob_grad - row_delta[..., None])).astype(BRAIN)
    score_grad, produced_total, second_parts = meet(score_grad, produced_total, second_parts)
    produced_total = shift_over(produced_total + produced_three, CTX, 1)
    second_half = ctx_parts(second_parts[0] + second_parts[1])
    down_parts = dp_parts(down_half, local_experts, units // dp_count)
    query_grad = (
        jnp.einsum("hqk,khd->qhd", score_grad, key_heads, preferred_element_type=FLOAT)
        * score_scale
    )
    key_grad = (
        jnp.einsum("hqk,qhd->khd", score_grad, query_heads, preferred_element_type=FLOAT)
        * score_scale
    )
    value_low = (
        jnp.einsum("hqk,qhd->khd", probs_low, attn_grad_heads, preferred_element_type=FLOAT)
        .astype(BRAIN)
        .reshape(length, columns)
    )
    query_grad, key_grad, value_low = meet(query_grad, key_grad, value_low)
    query_rot_grad = rotated_back(query_grad, cosine, sine_table).reshape(length, columns)
    key_rot_grad = rotated_back(key_grad, cosine, sine_table).reshape(length, columns)
    query_weighted = query_rot_grad * query_gain_own
    key_weighted = key_rot_grad * key_gain_own
    dots = jnp.stack(
        [jnp.sum(query_weighted * query_lin, axis=-1), jnp.sum(key_weighted * key_lin, axis=-1)]
    )
    dots = lax.psum(dots, CTX) * (1.0 / width)
    query_gain_grad = jnp.sum(query_rot_grad * query_lin * query_inverse, axis=0)
    key_gain_grad = jnp.sum(key_rot_grad * key_lin * key_inverse, axis=0)
    query_low = (
        query_inverse * query_weighted
        - query_lin * (query_inverse * query_inverse * query_inverse * dots[0][:, None])
    ).astype(BRAIN)
    key_low = (
        key_inverse * key_weighted
        - key_lin * (key_inverse * key_inverse * key_inverse * dots[1][:, None])
    ).astype(BRAIN)
    qkv_low = jnp.concatenate([query_low, key_low, value_low], axis=1)
    qkv_low, produced_total, out_weight_grad, first_half, second_half, down_parts, produced_zero = (
        meet(
            qkv_low,
            produced_total,
            out_weight_grad,
            first_half,
            second_half,
            down_parts,
            produced_zero,
        )
    )
    produced_total = produced_total + produced_zero
    mixed = hidden + produced_total.astype(FLOAT)
    down_weight_grad = (down_parts[0] + down_parts[1]).astype(FLOAT)
    out_weight_grad = sum(
        (
            part.astype(FLOAT)
            for part in ctx_parts(out_weight_grad)
        ),
        jnp.zeros(out_weight_grad.shape[1:], FLOAT),
    )

    attn_in_parts = times_transpose(qkv_low, qkv_weights)
    attn_gain_grad = jnp.sum(attn_in_parts * all_in.astype(FLOAT), axis=0) / attn_gain
    attn_in_low = attn_in_parts.astype(BRAIN)
    attn_in_slots = [
        lax.dynamic_slice_in_dim(attn_in_low, place * rows, rows, axis=0) for place in ring_places
    ]
    attn_in_total = shift_over(attn_in_slots[1], CTX, 1)
    attn_in_total = attn_in_total + attn_in_slots[2]
    attn_in_total = shift_over(attn_in_total, CTX, 1) + attn_in_slots[3]
    attn_in_grad = (shift_over(attn_in_total, CTX, 1) + attn_in_slots[0]).astype(FLOAT)
    gate_weight_grad, up_weight_grad = placed_grads(
        jnp.stack(ring_places).astype(jnp.int32), first_half + second_half, local_experts, units
    )

    empty = jnp.zeros((width,), FLOAT)
    small = jnp.concatenate(
        [
            jnp.stack(
                [
                    attn_gain_grad,
                    lax.dynamic_update_slice_in_dim(empty, query_gain_grad, first_column, axis=0),
                    lax.dynamic_update_slice_in_dim(empty, key_gain_grad, first_column, axis=0),
                    mlp_gain_grad,
                ],
                axis=0,
            ),
            router_grad.T,
        ],
        axis=0,
    )
    own_width = width // device_count
    small_count = 4 + experts_all
    small = small.reshape(small_count, device_count, own_width).transpose(1, 0, 2)
    small = small.reshape(ctx_count, dp_count, 2, 2, small_count * own_width // 128, 128)
    for axis, bit, mine, place in (
        (DP, 1, dp_at, 1),
        (EXPERT, far, expert_at // 2, 1),
        (EXPERT, near, expert_at % 2, 1),
    ):
        kept = lax.dynamic_index_in_dim(small, mine, axis=place, keepdims=False)
        given = lax.dynamic_index_in_dim(small, 1 - mine, axis=place, keepdims=False)
        small = kept + swap_over(given, axis, bit)
    small = sum(ctx_parts(small)).reshape(small_count, own_width)
    qkv_weight_grad = outer_sum(all_in, qkv_low).astype(BRAIN)
    qkv_weight_grad = lax.psum_scatter(
        qkv_weight_grad.reshape(ctx_count, width // ctx_count, 3 * columns),
        plane,
        scatter_dimension=1,
        tiled=True,
    )
    qkv_weight_grad = lax.all_to_all(qkv_weight_grad, CTX, split_axis=0, concat_axis=0, tiled=True)
    qkv_weight_grad = (
        qkv_weight_grad.reshape(ctx_count, own_width, 3, columns)
        .transpose(2, 1, 0, 3)
        .reshape(3, own_width, width)
        .astype(FLOAT)
    )
    input_part, _ = norm_backward(inputs, attn_inverse, attn_gain, attn_in_grad)
    input_grad = hidden_grad + input_part

    return (
        mixed.astype(BRAIN)[None],
        input_grad[None],
        qkv_weight_grad[0],
        qkv_weight_grad[1],
        qkv_weight_grad[2],
        out_weight_grad,
        small[0],
        small[1],
        small[2],
        small[3],
        small[4:].T,
        gate_weight_grad,
        up_weight_grad,
        down_weight_grad,
    )


def solution(mesh):
    sizes = mesh.shape
    if not (sizes[CTX] == 4 and sizes[EXPERT] == 4 and sizes[DP] == 2):
        return placed_over(mesh, plane_shards)

    return placed_over(mesh, line_shards)


def placed_over(mesh, shards):
    return jax.shard_map(
        shards,
        mesh=mesh,
        in_specs=(
            P((DP, EXPERT), CTX, None),
            P((DP, EXPERT), CTX, None),
            P(),
            P(),
            P(),
            P(),
            P(),
            P(),
            P(),
            P(),
            P(),
            P(EXPERT, None, None),
            P(EXPERT, None, None),
            P(EXPERT, None, None),
            P((DP, EXPERT), CTX, None),
        ),
        out_specs=(
            P((DP, EXPERT), CTX, None),
            P((DP, EXPERT), CTX, None),
            P((CTX, DP, EXPERT), None),
            P((CTX, DP, EXPERT), None),
            P((CTX, DP, EXPERT), None),
            P((CTX, DP, EXPERT), None),
            P((CTX, DP, EXPERT)),
            P((CTX, DP, EXPERT)),
            P((CTX, DP, EXPERT)),
            P((CTX, DP, EXPERT)),
            P((CTX, DP, EXPERT), None),
            P(EXPERT, (CTX, DP), None),
            P(EXPERT, (CTX, DP), None),
            P(EXPERT, (CTX, DP), None),
        ),
        check_vma=False,
    )
```

profile of v0, /device:TPU:0, one launch (start us, length us, event | category | flops | bytes accessed | tf_op | source)
XLA Modules:
  0.0 998.0 jit_solution(3252114502125319613)
XLA Ops:
  58.7 16.8 %all_gather.7 = f32[1024,2]{0,1:T(2,128)S(1)} all-gather(f32[256,2]{0,1:T(2,128)S(1)} %pad_maximum_fusion.7), channel_id=1, replica_groups=mesh['ctx'=4,'dp'=2,'expert'=4] {'ctx'}, dimensions={0}, use_global_device_ids=true | all-gather | bytes 10240 | tf_op jit(solution)/shard_map/all_gather | solution.py:669
  157.0 25.3 %all-to-all-done = bf16[4,256,512]{2,1,0:T(8,128)(2,1)S(1)} async-done(((bf16[4,256,512]{2,1,0:T(8,128)(2,1)}), bf16[4,256,512]{2,1,0:T(8,128)(2,1)S(1)}, u32[]{:S(2)}, u32[]{:S(2)}) %all-to-all-start) | async-done | bytes 1048608 | tf_op jit(solution)/shard_map/all_to_all | solution.py:746
  189.7 20.3 %collective-permute-done.14.refs_12_ = bf16[256,2048]{1,0:T(8,128)(2,1)} collective-permute-done((bf16[256,2048]{1,0:T(8,128)(2,1)}, bf16[256,2048]{1,0:T(8,128)(2,1)}, u32[]{:S(2)}, u32[]{:S(2)}) %collective-permute-start.14) | collective-permute-done | bytes 1048608 | tf_op jit(solution)/shard_map/ppermute | solution.py:617
  214.8 21.5 %collective-permute-done.15.refs_13_ = bf16[256,2048]{1,0:T(8,128)(2,1)} collective-permute-done((bf16[256,2048]{1,0:T(8,128)(2,1)}, bf16[256,2048]{1,0:T(8,128)(2,1)}, u32[]{:S(2)}, u32[]{:S(2)}) %collective-permute-start.15) | collective-permute-done | bytes 1048608 | tf_op jit(solution)/shard_map/ppermute | solution.py:612
  238.1 19.6 %collective-permute-done.11.far = bf16[256,2048]{1,0:T(8,128)(2,1)} collective-permute-done((bf16[256,2048]{1,0:T(8,128)(2,1)S(1)}, bf16[256,2048]{1,0:T(8,128)(2,1)}, u32[]{:S(2)}, u32[]{:S(2)}) %collective-permute-start.11) | collective-permute-done | bytes 1048608 | tf_op jit(solution)/shard_map/ppermute | solution.py:612
  259.0 26.0 %gathered_back.1 = (bf16[4096,2048]{1,0:T(8,128)(2,1)}, bf16[4096,1024]{1,0:T(8,128)(2,1)}) custom-call(bf16[256,2048]{1,0:T(8,128)(2,1)} %bitcast.2.refs_0_, bf16[256,2048]{1,0:T(8,128)(2,1)} %collective-permute-done.1.refs_1_, bf16[256,2048]{1,0:T(8,128)(2,1)} %collective-permute-done.4.refs_2_, bf16[256,2048]{1,0:T(8,128)(2,1)} %copy-done.99, ...), custom_call_target="tpu_custom_call" | custom-call | flops 17179869184 | bytes 50331648 | tf_op jit(solution)/shard_map/gathered_back/pallas_call | solution.py:554
  288.7 28.5 %expert_stage.4 = (bf16[256,2048]{1,0:T(8,128)(2,1)}, bf16[256,2048]{1,0:T(8,128)(2,1)}, bf16[256,2048]{1,0:T(8,128)(2,1)}, bf16[256,2048]{1,0:T(8,128)(2,1)}, f...) custom-call(s32[1]{0:T(128)} %bitcast.16.place, ...), custom_call_target="tpu_custom_call" | custom-call | flops 17179869184 | bytes 41943040 | tf_op jit(solution)/shard_map/expert_stage/pallas_call | solution.py:459
  325.4 28.6 %expert_stage.5 = (bf16[256,2048]{1,0:T(8,128)(2,1)}, bf16[256,2048]{1,0:T(8,128)(2,1)}, bf16[256,2048]{1,0:T(8,128)(2,1)}, bf16[256,2048]{1,0:T(8,128)(2,1)}, f...) custom-call(s32[1]{0:T(128)} %bitcast.16.place, ...), custom_call_target="tpu_custom_call", output_to_operand_aliasing={{5}: (9, {}), {6}: (10, {}), {7}: (11, {})} | custom-call | flops 17179869184 | bytes 41943040 | tf_op jit(solution)/shard_map/expert_stage/pallas_call | solution.py:459
  364.8 28.6 %expert_stage.6 = (bf16[256,2048]{1,0:T(8,128)(2,1)}, bf16[256,2048]{1,0:T(8,128)(2,1)}, bf16[256,2048]{1,0:T(8,128)(2,1)}, bf16[256,2048]{1,0:T(8,128)(2,1)}, f...) custom-call(s32[1]{0:T(128)} %bitcast.16.place, ...), custom_call_target="tpu_custom_call", output_to_operand_aliasing={{5}: (9, {}), {6}: (10, {}), {7}: (11, {})} | custom-call | flops 17179869184 | bytes 41943040 | tf_op jit(solution)/shard_map/expert_stage/pallas_call | solution.py:459
  408.8 28.9 %expert_stage.7 = (bf16[256,2048]{1,0:T(8,128)(2,1)}, bf16[256,2048]{1,0:T(8,128)(2,1)}, bf16[256,2048]{1,0:T(8,128)(2,1)}, bf16[256,2048]{1,0:T(8,128)(2,1)}, f...) custom-call(s32[1]{0:T(128)} %bitcast.16.place, ...), custom_call_target="tpu_custom_call", output_to_operand_aliasing={{5}: (9, {}), {6}: (10, {}), {7}: (11, {})} | custom-call | flops 17179869184 | bytes 41943040 | tf_op jit(solution)/shard_map/expert_stage/pallas_call | solution.py:459
  482.3 18.8 %collective-permute-done.51 = bf16[256,2048]{1,0:T(8,128)(2,1)S(1)} collective-permute-done((bf16[256,2048]{1,0:T(8,128)(2,1)S(1)}, bf16[256,2048]{1,0:T(8,128)(2,1)S(1)}, u32[]{:S(2)}, u32[]{:S(2)}) %collective-permute-start.51) | collective-permute-done | bytes 1048608 | tf_op jit(solution)/shard_map/ppermute | solution.py:612
  511.2 22.7 %fusion.10 = bf16[2048,1024]{1,0:T(8,128)(2,1)S(1)} fusion(bf16[4096,2048]{1,0:T(8,128)(2,1)} %get-tuple-element.362, bf16[4096,2048]{1,0:T(8,128)(2,1)} %get-tuple-element.363), kind=kOutput, calls=%fused_computation.20 | convolution fusion | flops 17181966336 | bytes 29360128 | tf_op jit(solution)/shard_map/dot_general | solution.py:61
  547.1 15.7 %collective-permute-done.61 = bf16[256,2048]{1,0:T(8,128)(2,1)S(1)} collective-permute-done((bf16[256,2048]{1,0:T(8,128)(2,1)S(1)}, bf16[256,2048]{1,0:T(8,128)(2,1)S(1)}, u32[]{:S(2)}, u32[]{:S(2)}) %collective-permute-start.61) | collective-permute-done | bytes 1048608 | tf_op jit(solution)/shard_map/ppermute | solution.py:617
  569.9 22.4 %fusion.13 = bf16[2048,1024]{1,0:T(8,128)(2,1)} fusion(bf16[4096,2048]{1,0:T(8,128)(2,1)S(1)} %bitcast.218, bf16[4096,2048]{1,0:T(8,128)(2,1)} %get-tuple-element.363), kind=kOutput, calls=%fused_computation.21 | convolution fusion | flops 17181966336 | bytes 29360128 | tf_op jit(solution)/shard_map/dot_general | solution.py:61
  620.1 23.9 %convolution_convert_fusion.2 = bf16[1024,2048]{1,0:T(8,128)(2,1)} fusion(bf16[4096,1024]{1,0:T(8,128)(2,1)} %get-tuple-element.343, bf16[4096,2048]{1,0:T(8,128)(2,1)} %get-tuple-element.386), kind=kOutput, calls=%fused_computation.22 | convolution fusion | flops 17181966336 | bytes 29360128 | tf_op jit(solution)/shard_map/dot_general | solution.py:61
  678.2 12.1 %multiply_convert_fusion = bf16[4,1024,1024]{1,2,0:T(8,128)(2,1)} fusion(bf16[1024,4,128]{0,2,1:T(8,128)(2,1)S(1)} %bitcast.231, f32[4,1024]{1,0:T(4,128)S(1)} %bitcast.260, f32[4,1024,1024]{1,2,0:T(8,128)} %get-tuple-element.498, f32[4,1024]{1,0:T(4,128)S(1)} %copy-done.91, f32[1024,1536]{1,0:T(8,128)} %copy-done.5), kind=kOutput, calls=%fused_computation.1 | convolution fusion | flops 1090519040 | bytes 27295744 | tf_op jit(solution)/shard_map/qhd,khd->hqk/dot_general | solution.py:946
  705.3 25.5 %collective-permute-done.71 = bf16[4,256,1024]{2,1,0:T(8,128)(2,1)} collective-permute-done((bf16[4,256,1024]{2,1,0:T(8,128)(2,1)}, bf16[4,256,1024]{2,1,0:T(8,128)(2,1)}, u32[]{:S(2)}, u32[]{:S(2)}) %collective-permute-start.71) | collective-permute-done | bytes 2097184 | tf_op jit(solution)/shard_map/ppermute | solution.py:612
  761.8 12.8 %psum.7 = f32[2,1024]{1,0:T(2,128)S(1)} all-reduce(f32[2,1024]{1,0:T(2,128)S(1)} %pad_maximum_fusion.6), channel_id=1, replica_groups=mesh['ctx'=4,'dp'=2,'expert'=4] {'ctx'}, use_global_device_ids=true, to_apply=%region_14.15 | all-reduce | flops 2048 | bytes 16384 | tf_op jit(solution)/shard_map/psum | solution.py:975
  788.9 23.4 %collective-permute-done.76.refs_5_ = bf16[256,1024]{1,0:T(8,128)(2,1)} collective-permute-done((bf16[256,1024]{1,0:T(8,128)(2,1)S(1)}, bf16[256,1024]{1,0:T(8,128)(2,1)}, u32[]{:S(2)}, u32[]{:S(2)}) %collective-permute-start.76) | collective-permute-done | bytes 524320 | tf_op jit(solution)/shard_map/ppermute | solution.py:617
  848.8 12.0 %collective-permute-start.81 = (bf16[256,2048]{1,0:T(8,128)(2,1)}, bf16[256,2048]{1,0:T(8,128)(2,1)}, u32[]{:S(2)}, u32[]{:S(2)}) collective-permute-start(bf16[256,2048]{1,0:T(8,128)(2,1)} %constant_dynamic-slice_fusion.4), channel_id=1, source_target_pairs={{0,8},{8,16},{16,24},{24,0},{1,9},{9,17},{17,25},{25,1},{2,10},{10... | collective-permute-start | bytes 3145736 | tf_op jit(solution)/shard_map/ppermute | solution.py:617
  871.5 12.3 %collective-permute-done.81 = bf16[256,2048]{1,0:T(8,128)(2,1)} collective-permute-done((bf16[256,2048]{1,0:T(8,128)(2,1)}, bf16[256,2048]{1,0:T(8,128)(2,1)}, u32[]{:S(2)}, u32[]{:S(2)}) %collective-permute-start.81) | collective-permute-done | bytes 1048608 | tf_op jit(solution)/shard_map/ppermute | solution.py:617
  901.7 13.3 %collective-permute-done.82 = bf16[256,2048]{1,0:T(8,128)(2,1)} collective-permute-done((bf16[256,2048]{1,0:T(8,128)(2,1)}, bf16[256,2048]{1,0:T(8,128)(2,1)}, u32[]{:S(2)}, u32[]{:S(2)}) %collective-permute-start.82) | collective-permute-done | bytes 1048608 | tf_op jit(solution)/shard_map/ppermute | solution.py:617
  934.2 19.0 %collective-permute-done.85 = bf16[64,2048]{1,0:T(8,128)(2,1)} collective-permute-done((bf16[64,2048]{1,0:T(8,128)(2,1)}, bf16[64,2048]{1,0:T(8,128)(2,1)}, u32[]{:S(2)}, u32[]{:S(2)}) %collective-permute-start.85) | collective-permute-done | bytes 262176 | tf_op jit(solution)/shard_map/ppermute | solution.py:617
  971.0 12.2 %all-to-all-done.2 = bf16[4,64,1536]{2,1,0:T(8,128)(2,1)} async-done(((bf16[4,64,1536]{2,1,0:T(8,128)(2,1)}), bf16[4,64,1536]{2,1,0:T(8,128)(2,1)}, u32[]{:S(2)}, u32[]{:S(2)}) %all-to-all-start.2) | async-done | bytes 786464 | tf_op jit(solution)/shard_map/all_to_all | solution.py:1059
  (585 shorter events, 491.7 us)
Async XLA Ops:
  7.2 88.4 %all-gather.2.cloned.1.call-start = ((), (), s32[]{:S(2)}) async-start(), calls=%async_computation.5 | async-start | bytes 5242880 | tf_op jit(solution)/shard_map/all_gather | solution.py:665
  97.4 52.0 %collective-permute-start.4 = (bf16[256,2048]{1,0:T(8,128)(2,1)}, bf16[256,2048]{1,0:T(8,128)(2,1)}, u32[]{:S(2)}, u32[]{:S(2)}) collective-permute-start(bf16[256,2048]{1,0:T(8,128)(2,1)} %bitcast.2.refs_0_), channel_id=1, source_target_pairs={{0,1},{1,0},{2,3},{3,2},{4,5},{5,4},{6,7},{7,6},{8,9},{9,8},{10,11... | collective-permute-start | bytes 3145736 | tf_op jit(solution)/shard_map/ppermute | solution.py:612
  214.3 43.5 %collective-permute-start.11 = (bf16[256,2048]{1,0:T(8,128)(2,1)S(1)}, bf16[256,2048]{1,0:T(8,128)(2,1)}, u32[]{:S(2)}, u32[]{:S(2)}) collective-permute-start(bf16[256,2048]{1,0:T(8,128)(2,1)S(1)} %multiply_convert_fusion.1.own), channel_id=1, source_target_pairs={{0,2},{1,3},{2,0},{3,1},{4,6},{5,7},{6,4},{7,5},{8,10},{9,11},{10,... | collective-permute-start | bytes 3145736 | tf_op jit(solution)/shard_map/ppermute | solution.py:612
  214.8 42.9 %collective-permute-start.12 = (bf16[256,2048]{1,0:T(8,128)(2,1)S(1)}, bf16[256,2048]{1,0:T(8,128)(2,1)}, u32[]{:S(2)}, u32[]{:S(2)}) collective-permute-start(bf16[256,2048]{1,0:T(8,128)(2,1)S(1)} %multiply_convert_fusion.1.own), channel_id=1, source_target_pairs={{0,1},{1,0},{2,3},{3,2},{4,5},{5,4},{6,7},{7,6},{8,9},{9,8},{10,11... | collective-permute-start | bytes 3145736 | tf_op jit(solution)/shard_map/ppermute | solution.py:612
  321.3 38.5 %collective-permute-start.29 = (bf16[256,2048]{1,0:T(8,128)(2,1)S(1)}, bf16[256,2048]{1,0:T(8,128)(2,1)}, u32[]{:S(2)}, u32[]{:S(2)}) collective-permute-start(bf16[256,2048]{1,0:T(8,128)(2,1)S(1)} %collective-permute-done.24.own), channel_id=1, source_target_pairs={{0,2},{1,3},{2,0},{3,1},{4,6},{5,7},{6,4},{7,5},{8,10},{9,11},{10,... | collective-permute-start | bytes 3145736 | tf_op jit(solution)/shard_map/ppermute | solution.py:612
  364.8 39.4 %collective-permute-start.36 = (bf16[256,2048]{1,0:T(8,128)(2,1)}, bf16[256,2048]{1,0:T(8,128)(2,1)S(1)}, u32[]{:S(2)}, u32[]{:S(2)}) collective-permute-start(bf16[256,2048]{1,0:T(8,128)(2,1)} %collective-permute-done.29.far), channel_id=1, source_target_pairs={{0,1},{1,0},{2,3},{3,2},{4,5},{5,4},{6,7},{7,6},{8,9},{9,8},{10,11... | collective-permute-start | bytes 3145736 | tf_op jit(solution)/shard_map/ppermute | solution.py:612
  568.4 44.3 %collective-permute-start.66 = (bf16[4,256,1024]{2,1,0:T(8,128)(2,1)}, bf16[4,256,1024]{2,1,0:T(8,128)(2,1)S(1)}, u32[]{:S(2)}, u32[]{:S(2)}) collective-permute-start(bf16[4,256,1024]{2,1,0:T(8,128)(2,1)} %get-tuple-element.444), channel_id=1, source_target_pairs={{0,4},{4,0},{1,5},{5,1},{2,6},{6,2},{3,7},{7,3},{8,12},{12,8},{9,1... | collective-permute-start | bytes 6291464 | tf_op jit(solution)/shard_map/ppermute | solution.py:612
  595.1 48.9 %collective-permute-start.68 = (bf16[256,2048]{1,0:T(8,128)(2,1)}, bf16[256,2048]{1,0:T(8,128)(2,1)}, u32[]{:S(2)}, u32[]{:S(2)}) collective-permute-start(bf16[256,2048]{1,0:T(8,128)(2,1)} %get-tuple-element.385), channel_id=1, source_target_pairs={{0,2},{1,3},{2,0},{3,1},{4,6},{5,7},{6,4},{7,5},{8,10},{9,11},{10,... | collective-permute-start | bytes 3145736 | tf_op jit(solution)/shard_map/ppermute | solution.py:612
  596.0 50.8 %collective-permute-start.67 = (bf16[256,2048]{1,0:T(8,128)(2,1)}, bf16[256,2048]{1,0:T(8,128)(2,1)}, u32[]{:S(2)}, u32[]{:S(2)}) collective-permute-start(bf16[256,2048]{1,0:T(8,128)(2,1)} %get-tuple-element.383), channel_id=1, source_target_pairs={{0,2},{1,3},{2,0},{3,1},{4,6},{5,7},{6,4},{7,5},{8,10},{9,11},{10,... | collective-permute-start | bytes 3145736 | tf_op jit(solution)/shard_map/ppermute | solution.py:612
  597.1 52.4 %collective-permute-start.69 = (bf16[256,2048]{1,0:T(8,128)(2,1)}, bf16[256,2048]{1,0:T(8,128)(2,1)}, u32[]{:S(2)}, u32[]{:S(2)}) collective-permute-start(bf16[256,2048]{1,0:T(8,128)(2,1)} %add.427), channel_id=1, source_target_pairs={{0,8},{8,16},{16,24},{24,0},{1,9},{9,17},{17,25},{25,1},{2,10},{10... | collective-permute-start | bytes 3145736 | tf_op jit(solution)/shard_map/ppermute | solution.py:617
  620.1 203.5 %reduce-scatter.3.cloned.1.call-start = ((), (), s32[]{:S(2)}) async-start(), calls=%async_computation.6 | async-start | bytes 9437184 | tf_op jit(solution)/shard_map/reduce_scatter | solution.py:937
  656.6 298.8 %reduce-scatter.5.cloned.1.call-start = ((), (), s32[]{:S(2)}) async-start(), calls=%async_computation.7 | async-start | bytes 7077888 | tf_op jit(solution)/shard_map/reduce_scatter | solution.py:1053
  661.5 69.3 %collective-permute-start.71 = (bf16[4,256,1024]{2,1,0:T(8,128)(2,1)}, bf16[4,256,1024]{2,1,0:T(8,128)(2,1)}, u32[]{:S(2)}, u32[]{:S(2)}) collective-permute-start(bf16[4,256,1024]{2,1,0:T(8,128)(2,1)} %get-tuple-element.442), channel_id=1, source_target_pairs={{0,4},{4,0},{1,5},{5,1},{2,6},{6,2},{3,7},{7,3},{8,12},{12,8},{9,1... | collective-permute-start | bytes 6291464 | tf_op jit(solution)/shard_map/ppermute | solution.py:612
  665.4 109.2 %collective-permute-start.73 = (bf16[256,1024]{1,0:T(8,128)(2,1)}, bf16[256,1024]{1,0:T(8,128)(2,1)}, u32[]{:S(2)}, u32[]{:S(2)}) collective-permute-start(bf16[256,1024]{1,0:T(8,128)(2,1)} %get-tuple-element.465), channel_id=1, source_target_pairs={{0,8},{8,16},{16,24},{24,0},{1,9},{9,17},{17,25},{25,1},{2,10},{10... | collective-permute-start | bytes 1572872 | tf_op jit(solution)/shard_map/ppermute | solution.py:617
  667.4 110.0 %collective-permute-start.74 = (bf16[256,1024]{1,0:T(8,128)(2,1)}, bf16[256,1024]{1,0:T(8,128)(2,1)}, u32[]{:S(2)}, u32[]{:S(2)}) collective-permute-start(bf16[256,1024]{1,0:T(8,128)(2,1)} %get-tuple-element.464), channel_id=1, source_target_pairs={{0,16},{8,24},{16,0},{24,8},{1,17},{9,25},{17,1},{25,9},{2,18},{10... | collective-permute-start | bytes 1572872 | tf_op jit(solution)/shard_map/ppermute | solution.py:617
  669.8 107.6 %collective-permute-start.75 = (bf16[256,1024]{1,0:T(8,128)(2,1)}, bf16[256,1024]{1,0:T(8,128)(2,1)}, u32[]{:S(2)}, u32[]{:S(2)}) collective-permute-start(bf16[256,1024]{1,0:T(8,128)(2,1)} %get-tuple-element.463), channel_id=1, source_target_pairs={{0,24},{8,0},{16,8},{24,16},{1,25},{9,1},{17,9},{25,17},{2,26},{10... | collective-permute-start | bytes 1572872 | tf_op jit(solution)/shard_map/ppermute | solution.py:617
  674.1 57.3 %collective-permute-start.70 = (bf16[256,2048]{1,0:T(8,128)(2,1)}, bf16[256,2048]{1,0:T(8,128)(2,1)}, u32[]{:S(2)}, u32[]{:S(2)}) collective-permute-start(bf16[256,2048]{1,0:T(8,128)(2,1)} %add.438), channel_id=1, source_target_pairs={{0,8},{8,16},{16,24},{24,0},{1,9},{9,17},{17,25},{25,1},{2,10},{10... | collective-permute-start | bytes 3145736 | tf_op jit(solution)/shard_map/ppermute | solution.py:617
  730.8 50.9 %collective-permute-start.80 = (bf16[256,2048]{1,0:T(8,128)(2,1)}, bf16[256,2048]{1,0:T(8,128)(2,1)}, u32[]{:S(2)}, u32[]{:S(2)}) collective-permute-start(bf16[256,2048]{1,0:T(8,128)(2,1)} %get-tuple-element.407), channel_id=1, source_target_pairs={{0,2},{1,3},{2,0},{3,1},{4,6},{5,7},{6,4},{7,5},{8,10},{9,11},{10,... | collective-permute-start | bytes 3145736 | tf_op jit(solution)/shard_map/ppermute | solution.py:612
  731.5 92.1 %collective-permute-start.79 = (bf16[4,128,2048]{2,1,0:T(8,128)(2,1)}, bf16[4,128,2048]{2,1,0:T(8,128)(2,1)}, u32[]{:S(2)}, u32[]{:S(2)}) collective-permute-start(bf16[4,128,2048]{2,1,0:T(8,128)(2,1)} %get-tuple-element.440), channel_id=1, source_target_pairs={{0,4},{4,0},{1,5},{5,1},{2,6},{6,2},{3,7},{7,3},{8,12},{12,8},{9,1... | collective-permute-start | bytes 6291464 | tf_op jit(solution)/shard_map/ppermute | solution.py:612
  774.6 49.0 %collective-permute-start.72 = (bf16[256,2048]{1,0:T(8,128)(2,1)}, bf16[256,2048]{1,0:T(8,128)(2,1)}, u32[]{:S(2)}, u32[]{:S(2)}) collective-permute-start(bf16[256,2048]{1,0:T(8,128)(2,1)} %add.441), channel_id=1, source_target_pairs={{0,8},{8,16},{16,24},{24,0},{1,9},{9,17},{17,25},{25,1},{2,10},{10... | collective-permute-start | bytes 3145736 | tf_op jit(solution)/shard_map/ppermute | solution.py:617
  777.4 46.2 %collective-permute-start.77 = (bf16[256,1024]{1,0:T(8,128)(2,1)S(1)}, bf16[256,1024]{1,0:T(8,128)(2,1)}, u32[]{:S(2)}, u32[]{:S(2)}) collective-permute-start(bf16[256,1024]{1,0:T(8,128)(2,1)S(1)} %get-tuple-element.460), channel_id=1, source_target_pairs={{0,16},{8,24},{16,0},{24,8},{1,17},{9,25},{17,1},{25,9},{2,18},{10... | collective-permute-start | bytes 1572872 | tf_op jit(solution)/shard_map/ppermute | solution.py:617
  781.6 42.0 %collective-permute-start.78 = (bf16[256,1024]{1,0:T(8,128)(2,1)S(1)}, bf16[256,1024]{1,0:T(8,128)(2,1)}, u32[]{:S(2)}, u32[]{:S(2)}) collective-permute-start(bf16[256,1024]{1,0:T(8,128)(2,1)S(1)} %get-tuple-element.459), channel_id=1, source_target_pairs={{0,24},{8,0},{16,8},{24,16},{1,25},{9,1},{17,9},{25,17},{2,26},{10... | collective-permute-start | bytes 1572872 | tf_op jit(solution)/shard_map/ppermute | solution.py:617
  895.4 38.8 %collective-permute-start.84 = (bf16[64,2048]{1,0:T(8,128)(2,1)}, bf16[64,2048]{1,0:T(8,128)(2,1)}, u32[]{:S(2)}, u32[]{:S(2)}) collective-permute-start(bf16[64,2048]{1,0:T(8,128)(2,1)} %get-tuple-element.475), channel_id=1, source_target_pairs={{0,8},{8,16},{16,24},{24,0},{1,9},{9,17},{17,25},{25,1},{2,10},{10... | collective-permute-start | bytes 786440 | tf_op jit(solution)/shard_map/ppermute | solution.py:617
  917.9 45.8 %collective-permute-start.83 = (bf16[256,2048]{1,0:T(8,128)(2,1)}, bf16[256,2048]{1,0:T(8,128)(2,1)}, u32[]{:S(2)}, u32[]{:S(2)}) collective-permute-start(bf16[256,2048]{1,0:T(8,128)(2,1)} %dynamic-slice_add_fusion.1), channel_id=1, source_target_pairs={{0,8},{8,16},{16,24},{24,0},{1,9},{9,17},{17,25},{25,1},{2,10},{10... | collective-permute-start | bytes 3145736 | tf_op jit(solution)/shard_map/ppermute | solution.py:617
  (181 other events, 3572.3 us)
Sparse Core Ops, SparseCore 0:
  12.0 83.5 all-gather.1
  656.7 104.7 reduce-scatter.2
  835.3 76.8 reduce-scatter.4
where the time goes:
time: 1010 us; the launch traced here: 998 us
  waiting for transfers between devices  271 us (27%)
  matrix products  210 us (21%)
  Pallas kernels  147 us (15%)
  other arithmetic  131 us (13%)
  local copies, waits for them, and re-layouts  96.8 us (10%)
  starting transfers between devices  96.8 us (10%)
  blocking collectives  29.5 us (3%)
  between operations  16.2 us (2%)
    ppermute x33, waiting for transfers between devices, shift_over(): lax.ppermute(values, axis, [(at, (at + steps) % count) for at in range(co...  123 us
    pallas_call x4, Pallas kernels, expert_stage(): pl.pallas_call(functools.partial(stage_body, slot, count, units), grid_sp...  115 us
    ppermute x60, waiting for transfers between devices, swap_over(): return lax.ppermute(values, axis, [(at, at ^ bit) for at in range(count)])  101 us
    dot_general x6, matrix products, outer_sum(): lax.dot_general(left, right, (((0,), (0,)), ((), ())), preferred_element_...  87.9 us
    dot_general x13, matrix products, times(): return jnp.dot(left, right, preferred_element_type=FLOAT)  60.2 us
    ppermute x33, starting transfers between devices, shift_over(): lax.ppermute(values, axis, [(at, (at + steps) % count) for at in range(co...  43.9 us
    ppermute x60, starting transfers between devices, swap_over(): return lax.ppermute(values, axis, [(at, at ^ bit) for at in range(count)])  34.2 us
    pallas_call x1, Pallas kernels, gathered_back(): pl.pallas_call(functools.partial(back_body, count), grid=(count,), in_spe...  26 us
  transfers between devices with their start and end apart: 99, of which 25 were waited for; matrix products, arithmetic and copies ran while one was open for 36% of the time, Pallas kernels for 15%

commit v1 on v0

--- a/solution.py
+++ b/solution.py
@@ -19,7 +19,7 @@
 DP = "dp"
 EXPERT = "expert"
 OWN, FAR, NEAR, BOTH, GATES, UP_BOTH, BACK, STAGE = range(8)
-NEAR_SUM, FAR_SUM, MADE, RING, HALF = range(8, 13)
+NEAR_SUM, FAR_SUM, MADE, RING, HALF, DGATE = range(8, 14)
 
 
 def norm_inverse(values):
@@ -398,7 +398,8 @@
             sigmoid = jax.nn.sigmoid(gate_pre)
             silu = gate_pre * sigmoid
             activated = silu * up_pre
-            weighted_out[part, :] = (gate * activated).astype(BRAIN)
+            inner = pl.ds(pl.multiple_of(lax.rem(at, 2) * rows, rows), rows)
+            weighted_out[lax.div(at, 2), inner, :] = (gate * activated).astype(BRAIN)
             gate_grad = jnp.sum(down_back * activated, axis=1, keepdims=True)
             gate_grads_out[part, :] += jnp.where(wanted, gate_grad, 0.0)
             act_grad = gate * down_back
@@ -448,12 +449,12 @@
     whole_specs = [
         anywhere,
         pl.BlockSpec((stage_rows, both_units), lambda i, p: (slot, first_part(i))),
-        pl.BlockSpec((stage_rows, units), lambda i, p: (slot, first_part(i))),
+        pl.BlockSpec((2, stage_rows // 2, units), lambda i, p: (0, slot, first_part(i))),
     ]
     whole_shapes = [
         jax.ShapeDtypeStruct((all_rows, width), BRAIN),
         jax.ShapeDtypeStruct((all_rows, count * both_units), BRAIN),
-        jax.ShapeDtypeStruct((all_rows, count * units), BRAIN),
+        jax.ShapeDtypeStruct((2, all_rows // 2, count * units), BRAIN),
     ]
     previous = () if buffers is None else tuple(buffers)
     return pl.pallas_call(
@@ -510,11 +511,14 @@
         ]
 
     def outgoing(slot):
-        return pltpu.make_async_copy(
-            held.at[slot % 2],
-            rows_out.at[pl.ds(slot * 4 * rows, 4 * rows), :],
-            out_sems.at[slot % 2],
-        )
+        return [
+            pltpu.make_async_copy(
+                held.at[slot % 2, pl.ds(half * 2 * rows, 2 * rows), :],
+                rows_out.at[pl.ds((half * count + slot) * 2 * rows, 2 * rows), :],
+                out_sems.at[slot % 2, half],
+            )
+            for half in (0, 1)
+        ]
 
     for slot in range(count):
 
@@ -524,13 +528,15 @@
                 for copy in incoming(0):
                     copy.start()
             if slot > 0:
-                outgoing(slot - 1).wait()
+                for copy in outgoing(slot - 1):
+                    copy.wait()
             if slot + 1 < count:
                 for copy in incoming(slot + 1):
                     copy.start()
             for copy in incoming(slot):
                 copy.wait()
-            outgoing(slot).start()
+            for copy in outgoing(slot):
+                copy.start()
 
     def one(at, carry):
         part = pl.ds(pl.multiple_of(at * rows, rows), rows)
@@ -543,7 +549,8 @@
 
     @pl.when(step == count - 1)
     def _():
-        outgoing(count - 1).wait()
+        for copy in outgoing(count - 1):
+            copy.wait()
 
 
 def gathered_back(blocks, weights):
@@ -559,7 +566,7 @@
         scratch_shapes=[
             pltpu.VMEM((2, 4 * rows, width), BRAIN),
             pltpu.SemaphoreType.DMA((2, 4)),
-            pltpu.SemaphoreType.DMA((2,)),
+            pltpu.SemaphoreType.DMA((2, 2)),
         ],
         out_shape=[
             jax.ShapeDtypeStruct((4 * rows * count, width), BRAIN),
@@ -792,7 +799,7 @@
     moved_own = [expert_in]
     moved_far, moved_near, moved_both = [], [], []
     gate_slots, stages, near_sums, far_sums, half_grads = [], [], [], [], []
-    buffers = produced = sent = total = total_gate = None
+    buffers = produced = sent = total = gate_parts = None
     gate_half = padded_gates
     for tick in range(ctx_count + 5):
         slot = tick - 2
@@ -832,38 +839,41 @@
             )
         if 0 <= slot - 1 < ctx_count:
             grads = stages[slot - 1]
-            gate_part = grads[4].astype(BRAIN)
             fresh[NEAR_SUM] = (
                 grads[0] + swap_over(grads[2], EXPERT, near),
                 grads[1] + swap_over(grads[3], EXPERT, near),
-                gate_part[: 2 * rows] + swap_over(gate_part[2 * rows :], EXPERT, near),
             )
         if 0 <= slot - 2 < ctx_count:
             pair = near_sums[slot - 2]
-            fresh[FAR_SUM] = (
-                pair[0] + swap_over(pair[1], EXPERT, far),
-                pair[2][:rows] + swap_over(pair[2][rows:], EXPERT, far),
+            fresh[FAR_SUM] = pair[0] + swap_over(pair[1], EXPERT, far)
+        if tick == ctx_count + 2:
+            total = far_sums[1]
+            all_rows, all_pre_grads, all_weighted = buffers
+            fresh[MADE] = [times(all_weighted[half], down_weights).astype(BRAIN) for half in (0, 1)]
+            gate_parts = jnp.stack([stage[4] for stage in stages]).astype(BRAIN)
+            fresh[DGATE] = gate_parts[:, : 2 * rows] + swap_over(
+                gate_parts[:, 2 * rows :], EXPERT, near
             )
-        if tick == ctx_count + 2:
-            total, total_gate = far_sums[1]
-            all_rows, all_pre_grads, all_weighted = buffers
+        if tick >= ctx_count + 2:
+            fresh[RING] = shift_over(total, CTX, 1)
+        if tick == ctx_count + 3:
+            taken = swap_over(produced[1], EXPERT, near)
             fresh[MADE] = [
                 [
-                    times(
-                        all_weighted[(4 * at + 2 * part) * rows :][: 2 * rows], down_weights
-                    ).astype(BRAIN)
-                    for part in (0, 1)
+                    produced[0][place : place + rows] + taken[place : place + rows]
+                    for place in (2 * at * rows, (2 * at + 1) * rows)
                 ]
                 for at in range(ctx_count)
             ]
-        if tick >= ctx_count + 2:
-            fresh[RING] = (shift_over(total, CTX, 1), shift_over(total_gate, CTX, 1))
-        if tick == ctx_count + 3:
-            fresh[MADE] = []
-            for kept, given in produced:
-                taken = swap_over(given, EXPERT, near)
-                fresh[MADE].append((kept[:rows] + taken[:rows], kept[rows:] + taken[rows:]))
+            fresh[DGATE] = gate_parts[:, :rows] + swap_over(gate_parts[:, rows:], EXPERT, far)
         if tick == ctx_count + 4:
+            fresh[DGATE] = sum(
+                (
+                    shift_over(gate_parts[at], CTX, ctx_count - at).astype(FLOAT)
+                    for at in range(1, ctx_count)
+                ),
+                gate_parts[0].astype(FLOAT),
+            )
             fresh[MADE] = [produced[1][0] + swap_over(produced[1][1], EXPERT, far), produced]
             first_parts = dp_parts(half_grads[0], ctx_count, grad_rows)
         if tick >= ctx_count + 3:
@@ -895,14 +905,15 @@
             far_sums.append(fresh[FAR_SUM])
         if RING in fresh:
             following = far_sums[(tick - ctx_count) % ctx_count]
-            total = fresh[RING][0] + following[0]
-            total_gate = fresh[RING][1] + following[1]
+            total = fresh[RING] + following
+        if DGATE in fresh:
+            gate_parts = fresh[DGATE]
         if MADE in fresh:
             produced = fresh[MADE]
         if HALF in fresh:
             half_grads.append(fresh[HALF])
     expert_in_grad = total.astype(FLOAT)
-    gate_grads = total_gate[:, :experts_all].astype(FLOAT)
+    gate_grads = gate_parts[:, :experts_all]
     produced_total, produced = produced
 
     prob_grads = jnp.where(chosen, gate_grads, 0.0)
@@ -928,7 +939,9 @@
         tiled=True,
     ).reshape(length, columns)
     first_half = ctx_parts(first_parts[0] + first_parts[1])
-    down_half = outer_sum(all_weighted, all_upstream).astype(BRAIN)
+    down_half = outer_sum(
+        all_weighted.reshape(all_upstream.shape[0], hidden_units), all_upstream
+    ).astype(BRAIN)
     attn_grad, produced_two, produced_three, down_half, produced, hidden_low, produced_total = meet(
         attn_grad, produced_two, produced_three, down_half, produced, hidden_low, produced_total
     )
@@ -1048,7 +1061,6 @@
         kept = lax.dynamic_index_in_dim(small, mine, axis=place, keepdims=False)
         given = lax.dynamic_index_in_dim(small, 1 - mine, axis=place, keepdims=False)
         small = kept + swap_over(given, axis, bit)
-    small = sum(ctx_parts(small)).reshape(small_count, own_width)
     qkv_weight_grad = outer_sum(all_in, qkv_low).astype(BRAIN)
     qkv_weight_grad = lax.psum_scatter(
         qkv_weight_grad.reshape(ctx_count, width // ctx_count, 3 * columns),
@@ -1056,7 +1068,9 @@
         scatter_dimension=1,
         tiled=True,
     )
+    qkv_weight_grad, small = meet(qkv_weight_grad, small)
     qkv_weight_grad = lax.all_to_all(qkv_weight_grad, CTX, split_axis=0, concat_axis=0, tiled=True)
+    small = sum(ctx_parts(small)).reshape(small_count, own_width)
     qkv_weight_grad = (
         qkv_weight_grad.reshape(ctx_count, own_width, 3, columns)
         .transpose(2, 1, 0, 3)

time: 1010 us -> 986 us (0.976)
  matrix products: 210 us -> 195 us
    ppermute x33, starting transfers between devices: 43.9 us -> 56.8 us  [shift_over(): lax.ppermute(values, axis, [(at, (at + steps) % count) for at in range(co...]
    all_to_all x1, waiting for transfers between devices: 12.2 us -> 0.01 us  [line_shards(): lax.all_to_all(qkv_weight_grad, CTX, split_axis=0, concat_axis=0, tiled=T...]
    dot_general x13 -> x7, matrix products: 60.2 us -> 49.7 us  [times(): return jnp.dot(left, right, preferred_element_type=FLOAT)]
    ppermute x60 -> x51, starting transfers between devices: 34.2 us -> 31.9 us  [swap_over(): return lax.ppermute(values, axis, [(at, at ^ bit) for at in range(count)])]
    add x20 -> x10, other arithmetic: 21.1 us -> 19.4 us  [the longest x1 9.25 us: line_shards(): produced[0][place:place + rows] + taken[place:place + rows]]
    ppermute x60 -> x51, waiting for transfers between devices: 101 us -> 100 us  [swap_over(): return lax.ppermute(values, axis, [(at, at ^ bit) for at in range(count)])]
  transfers between devices with their start and end apart: 99 -> 90, of which waited for: 25 -> 21; matrix products, arithmetic and copies ran while one was open for 36% -> 38% of each run, Pallas kernels for 15% -> 15%
where the time goes in v1:
time: 986 us; the launch traced here: 977 us
  waiting for transfers between devices  261 us (26%)
  matrix products  195 us (20%)
  Pallas kernels  147 us (15%)
  other arithmetic  132 us (13%)
  starting transfers between devices  105 us (11%)
  local copies, waits for them, and re-layouts  90.8 us (9%)
  blocking collectives  29.7 us (3%)
  between operations  16.1 us (2%)
    ppermute x33, waiting for transfers between devices, shift_over(): lax.ppermute(values, axis, [(at, (at + steps) % count) for at in range(co...  126 us
    pallas_call x4, Pallas kernels, expert_stage(): pl.pallas_call(functools.partial(stage_body, slot, count, units), grid_sp...  115 us
    ppermute x51, waiting for transfers between devices, swap_over(): return lax.ppermute(values, axis, [(at, at ^ bit) for at in range(count)])  100 us
    dot_general x6, matrix products, outer_sum(): lax.dot_general(left, right, (((0,), (0,)), ((), ())), preferred_element_...  88.9 us
    ppermute x33, starting transfers between devices, shift_over(): lax.ppermute(values, axis, [(at, (at + steps) % count) for at in range(co...  56.8 us
    dot_general x7, matrix products, times(): return jnp.dot(left, right, preferred_element_type=FLOAT)  49.7 us
    ppermute x51, starting transfers between devices, swap_over(): return lax.ppermute(values, axis, [(at, at ^ bit) for at in range(count)])  31.9 us
    pallas_call x1, Pallas kernels, gathered_back(): pl.pallas_call(functools.partial(back_body, count), grid=(count,), in_spe...  26 us
  transfers between devices with their start and end apart: 90, of which 21 were waited for; matrix products, arithmetic and copies ran while one was open for 38% of the time, Pallas kernels for 15%

profile of v1, /device:TPU:0, one launch (start us, length us, event | category | flops | bytes accessed | tf_op | source)
XLA Modules:
  0.0 977.1 jit_solution(3724242393233122684)
XLA Ops:
  22.3 11.6 %copy.149 = bf16[4,512,2048]{2,1,0:T(8,128)(2,1)} copy(bf16[4,512,2048]{1,2,0:T(8,128)(2,1)} %get-tuple-element.420) | data formatting | bytes 16777216 | tf_op jit(solution)/shard_map/transpose | solution.py:695
  58.4 17.0 %all_gather.7 = f32[1024,2]{0,1:T(2,128)S(1)} all-gather(f32[256,2]{0,1:T(2,128)S(1)} %pad_maximum_fusion.8), channel_id=1, replica_groups=mesh['ctx'=4,'dp'=2,'expert'=4] {'ctx'}, dimensions={0}, use_global_device_ids=true | all-gather | bytes 10240 | tf_op jit(solution)/shard_map/all_gather | solution.py:676
  124.3 11.8 %fusion.72 = (f32[4,1024]{1,0:T(4,128)S(1)}, f32[4,1024,1024]{1,2,0:T(8,128)}) fusion(pred[1024,1024]{0,1:T(8,128)(4,1)} %iota_compare_fusion, bf16[1024,4,128]{0,2,1:T(8,128)(2,1)} %get-tuple-element.210, bf16[1024,4,128]{0,2,1:T(8,128)(2,1)} %get-tuple-element.211), kind=kOutput, calls=%fused_computation.211 | convolution fusion | flops 1090520064 | bytes 19939328 | tf_op jit(solution)/shard_map/sub | solution.py:744
  157.2 25.3 %all-to-all-done = bf16[4,256,512]{2,1,0:T(8,128)(2,1)S(1)} async-done(((bf16[4,256,512]{2,1,0:T(8,128)(2,1)}), bf16[4,256,512]{2,1,0:T(8,128)(2,1)S(1)}, u32[]{:S(2)}, u32[]{:S(2)}) %all-to-all-start) | async-done | bytes 1048608 | tf_op jit(solution)/shard_map/all_to_all | solution.py:753
  189.6 20.3 %collective-permute-done.14.refs_12_ = bf16[256,2048]{1,0:T(8,128)(2,1)} collective-permute-done((bf16[256,2048]{1,0:T(8,128)(2,1)}, bf16[256,2048]{1,0:T(8,128)(2,1)}, u32[]{:S(2)}, u32[]{:S(2)}) %collective-permute-start.14) | collective-permute-done | bytes 1048608 | tf_op jit(solution)/shard_map/ppermute | solution.py:624
  214.8 21.5 %collective-permute-done.15.refs_13_ = bf16[256,2048]{1,0:T(8,128)(2,1)} collective-permute-done((bf16[256,2048]{1,0:T(8,128)(2,1)}, bf16[256,2048]{1,0:T(8,128)(2,1)}, u32[]{:S(2)}, u32[]{:S(2)}) %collective-permute-start.15) | collective-permute-done | bytes 1048608 | tf_op jit(solution)/shard_map/ppermute | solution.py:619
  238.1 19.6 %collective-permute-done.11.far = bf16[256,2048]{1,0:T(8,128)(2,1)} collective-permute-done((bf16[256,2048]{1,0:T(8,128)(2,1)S(1)}, bf16[256,2048]{1,0:T(8,128)(2,1)}, u32[]{:S(2)}, u32[]{:S(2)}) %collective-permute-start.11) | collective-permute-done | bytes 1048608 | tf_op jit(solution)/shard_map/ppermute | solution.py:619
  258.9 26.0 %gathered_back.1 = (bf16[4096,2048]{1,0:T(8,128)(2,1)}, bf16[4096,1024]{1,0:T(8,128)(2,1)}) custom-call(bf16[256,2048]{1,0:T(8,128)(2,1)} %bitcast.2.refs_0_, bf16[256,2048]{1,0:T(8,128)(2,1)} %collective-permute-done.1.refs_1_, bf16[256,2048]{1,0:T(8,128)(2,1)} %collective-permute-done.4.refs_2_, bf16[256,2048]{1,0:T(8,128)(2,1)} %copy-done.85, ...), custom_call_target="tpu_custom_call" | custom-call | flops 17179869184 | bytes 50331648 | tf_op jit(solution)/shard_map/gathered_back/pallas_call | solution.py:561
  289.6 28.7 %expert_stage.4 = (bf16[256,2048]{1,0:T(8,128)(2,1)}, bf16[256,2048]{1,0:T(8,128)(2,1)}, bf16[256,2048]{1,0:T(8,128)(2,1)}, bf16[256,2048]{1,0:T(8,128)(2,1)}, f...) custom-call(s32[1]{0:T(128)} %bitcast.16.place, ...), custom_call_target="tpu_custom_call" | custom-call | flops 17179869184 | bytes 41943040 | tf_op jit(solution)/shard_map/expert_stage/pallas_call | solution.py:460
  325.4 28.7 %expert_stage.5 = (bf16[256,2048]{1,0:T(8,128)(2,1)}, bf16[256,2048]{1,0:T(8,128)(2,1)}, bf16[256,2048]{1,0:T(8,128)(2,1)}, bf16[256,2048]{1,0:T(8,128)(2,1)}, f...) custom-call(s32[1]{0:T(128)} %bitcast.16.place, ...), custom_call_target="tpu_custom_call", output_to_operand_aliasing={{5}: (9, {}), {6}: (10, {}), {7}: (11, {})} | custom-call | flops 17179869184 | bytes 41943040 | tf_op jit(solution)/shard_map/expert_stage/pallas_call | solution.py:460
  361.4 28.6 %expert_stage.6 = (bf16[256,2048]{1,0:T(8,128)(2,1)}, bf16[256,2048]{1,0:T(8,128)(2,1)}, bf16[256,2048]{1,0:T(8,128)(2,1)}, bf16[256,2048]{1,0:T(8,128)(2,1)}, f...) custom-call(s32[1]{0:T(128)} %bitcast.16.place, ...), custom_call_target="tpu_custom_call", output_to_operand_aliasing={{5}: (9, {}), {6}: (10, {}), {7}: (11, {})} | custom-call | flops 17179869184 | bytes 41943040 | tf_op jit(solution)/shard_map/expert_stage/pallas_call | solution.py:460
  400.9 28.7 %expert_stage.7 = (bf16[256,2048]{1,0:T(8,128)(2,1)}, bf16[256,2048]{1,0:T(8,128)(2,1)}, bf16[256,2048]{1,0:T(8,128)(2,1)}, bf16[256,2048]{1,0:T(8,128)(2,1)}, f...) custom-call(s32[1]{0:T(128)} %bitcast.16.place, ...), custom_call_target="tpu_custom_call", output_to_operand_aliasing={{5}: (9, {}), {6}: (10, {}), {7}: (11, {})} | custom-call | flops 17179869184 | bytes 41943040 | tf_op jit(solution)/shard_map/expert_stage/pallas_call | solution.py:460
  473.9 23.7 %fusion.14 = bf16[2048,1024]{1,0:T(8,128)(2,1)} fusion(bf16[4096,2048]{1,0:T(8,128)(2,1)} %get-tuple-element.337, bf16[4096,2048]{1,0:T(8,128)(2,1)} %get-tuple-element.338), kind=kOutput, calls=%fused_computation.26 | convolution fusion | flops 17181966336 | bytes 29360128 | tf_op jit(solution)/shard_map/dot_general | solution.py:61
  513.5 22.5 %fusion.17 = bf16[2048,1024]{1,0:T(8,128)(2,1)} fusion(bf16[4096,2048]{1,0:T(8,128)(2,1)S(1)} %bitcast.236, bf16[4096,2048]{1,0:T(8,128)(2,1)} %get-tuple-element.338), kind=kOutput, calls=%fused_computation.27 | convolution fusion | flops 17181966336 | bytes 29360128 | tf_op jit(solution)/shard_map/dot_general | solution.py:61
  560.3 29.1 %collective-permute-done.57 = bf16[4,256,1024]{2,1,0:T(8,128)(2,1)S(1)} collective-permute-done((bf16[4,256,1024]{2,1,0:T(8,128)(2,1)S(1)}, bf16[4,256,1024]{2,1,0:T(8,128)(2,1)S(1)}, u32[]{:S(2)}, u32[]{:S(2)}) %collective-permute-start.57) | collective-permute-done | bytes 2097184 | tf_op jit(solution)/shard_map/ppermute | solution.py:619
  596.6 23.9 %convolution_convert_fusion.4 = bf16[1024,2048]{1,0:T(8,128)(2,1)} fusion(bf16[4096,1024]{1,0:T(8,128)(2,1)} %bitcast.241, bf16[4096,2048]{1,0:T(8,128)(2,1)} %get-tuple-element.360), kind=kOutput, calls=%fused_computation.28 | convolution fusion | flops 17181966336 | bytes 29360128 | tf_op jit(solution)/shard_map/dot_general | solution.py:61
  654.5 12.0 %multiply_convert_fusion = bf16[4,1024,1024]{1,2,0:T(8,128)(2,1)} fusion(bf16[1024,4,128]{0,2,1:T(8,128)(2,1)S(1)} %bitcast.252, f32[4,1024]{1,0:T(4,128)S(1)} %bitcast.281, f32[4,1024,1024]{1,2,0:T(8,128)} %get-tuple-element.477, f32[4,1024]{1,0:T(4,128)S(1)} %copy-done.81, f32[1024,1536]{1,0:T(8,128)} %copy-done.5), kind=kOutput, calls=%fused_computation.1 | convolution fusion | flops 1090519040 | bytes 27295744 | tf_op jit(solution)/shard_map/qhd,khd->hqk/dot_general | solution.py:959
  681.5 25.8 %collective-permute-done.62 = bf16[4,256,1024]{2,1,0:T(8,128)(2,1)} collective-permute-done((bf16[4,256,1024]{2,1,0:T(8,128)(2,1)}, bf16[4,256,1024]{2,1,0:T(8,128)(2,1)}, u32[]{:S(2)}, u32[]{:S(2)}) %collective-permute-start.62) | collective-permute-done | bytes 2097184 | tf_op jit(solution)/shard_map/ppermute | solution.py:619
  738.3 12.8 %psum.7 = f32[2,1024]{1,0:T(2,128)S(1)} all-reduce(f32[2,1024]{1,0:T(2,128)S(1)} %pad_maximum_fusion.7), channel_id=1, replica_groups=mesh['ctx'=4,'dp'=2,'expert'=4] {'ctx'}, use_global_device_ids=true, to_apply=%region_14.15 | all-reduce | flops 2048 | bytes 16384 | tf_op jit(solution)/shard_map/psum | solution.py:988
  765.4 25.2 %collective-permute-done.67.refs_5_ = bf16[256,1024]{1,0:T(8,128)(2,1)} collective-permute-done((bf16[256,1024]{1,0:T(8,128)(2,1)S(1)}, bf16[256,1024]{1,0:T(8,128)(2,1)}, u32[]{:S(2)}, u32[]{:S(2)}) %collective-permute-start.67) | collective-permute-done | bytes 524320 | tf_op jit(solution)/shard_map/ppermute | solution.py:624
  790.6 11.8 %collective-permute-done.68.refs_6_ = bf16[256,1024]{1,0:T(8,128)(2,1)} collective-permute-done((bf16[256,1024]{1,0:T(8,128)(2,1)S(1)}, bf16[256,1024]{1,0:T(8,128)(2,1)}, u32[]{:S(2)}, u32[]{:S(2)}) %collective-permute-start.68) | collective-permute-done | bytes 524320 | tf_op jit(solution)/shard_map/ppermute | solution.py:624
  828.1 11.9 %collective-permute-start.72 = (bf16[256,2048]{1,0:T(8,128)(2,1)}, bf16[256,2048]{1,0:T(8,128)(2,1)}, u32[]{:S(2)}, u32[]{:S(2)}) collective-permute-start(bf16[256,2048]{1,0:T(8,128)(2,1)} %constant_dynamic-slice_fusion.4), channel_id=1, source_target_pairs={{0,8},{8,16},{16,24},{24,0},{1,9},{9,17},{17,25},{25,1},{2,10},{10... | collective-permute-start | bytes 3145736 | tf_op jit(solution)/shard_map/ppermute | solution.py:624
  850.3 13.6 %collective-permute-done.72 = bf16[256,2048]{1,0:T(8,128)(2,1)} collective-permute-done((bf16[256,2048]{1,0:T(8,128)(2,1)}, bf16[256,2048]{1,0:T(8,128)(2,1)}, u32[]{:S(2)}, u32[]{:S(2)}) %collective-permute-start.72) | collective-permute-done | bytes 1048608 | tf_op jit(solution)/shard_map/ppermute | solution.py:624
  874.1 28.2 %collective-permute-done.73 = bf16[256,2048]{1,0:T(8,128)(2,1)S(1)} collective-permute-done((bf16[256,2048]{1,0:T(8,128)(2,1)S(1)}, bf16[256,2048]{1,0:T(8,128)(2,1)S(1)}, u32[]{:S(2)}, u32[]{:S(2)}) %collective-permute-start.73) | collective-permute-done | bytes 1048608 | tf_op jit(solution)/shard_map/ppermute | solution.py:624
  (521 shorter events, 452.9 us)
Async XLA Ops:
  7.2 88.3 %all-gather.2.cloned.1.call-start = ((), (), s32[]{:S(2)}) async-start(), calls=%async_computation.5 | async-start | bytes 5242880 | tf_op jit(solution)/shard_map/all_gather | solution.py:672
  97.5 52.0 %collective-permute-start.4 = (bf16[256,2048]{1,0:T(8,128)(2,1)}, bf16[256,2048]{1,0:T(8,128)(2,1)}, u32[]{:S(2)}, u32[]{:S(2)}) collective-permute-start(bf16[256,2048]{1,0:T(8,128)(2,1)} %bitcast.2.refs_0_), channel_id=1, source_target_pairs={{0,1},{1,0},{2,3},{3,2},{4,5},{5,4},{6,7},{7,6},{8,9},{9,8},{10,11... | collective-permute-start | bytes 3145736 | tf_op jit(solution)/shard_map/ppermute | solution.py:619
  214.2 43.4 %collective-permute-start.11 = (bf16[256,2048]{1,0:T(8,128)(2,1)S(1)}, bf16[256,2048]{1,0:T(8,128)(2,1)}, u32[]{:S(2)}, u32[]{:S(2)}) collective-permute-start(bf16[256,2048]{1,0:T(8,128)(2,1)S(1)} %multiply_convert_fusion.1.own), channel_id=1, source_target_pairs={{0,2},{1,3},{2,0},{3,1},{4,6},{5,7},{6,4},{7,5},{8,10},{9,11},{10,... | collective-permute-start | bytes 3145736 | tf_op jit(solution)/shard_map/ppermute | solution.py:619
  214.8 42.9 %collective-permute-start.12 = (bf16[256,2048]{1,0:T(8,128)(2,1)S(1)}, bf16[256,2048]{1,0:T(8,128)(2,1)}, u32[]{:S(2)}, u32[]{:S(2)}) collective-permute-start(bf16[256,2048]{1,0:T(8,128)(2,1)S(1)} %multiply_convert_fusion.1.own), channel_id=1, source_target_pairs={{0,1},{1,0},{2,3},{3,2},{4,5},{5,4},{6,7},{7,6},{8,9},{9,8},{10,11... | collective-permute-start | bytes 3145736 | tf_op jit(solution)/shard_map/ppermute | solution.py:619
  542.9 46.4 %collective-permute-start.57 = (bf16[4,256,1024]{2,1,0:T(8,128)(2,1)S(1)}, bf16[4,256,1024]{2,1,0:T(8,128)(2,1)S(1)}, u32[]{:S(2)}, u32[]{:S(2)}) collective-permute-start(bf16[4,256,1024]{2,1,0:T(8,128)(2,1)S(1)} %get-tuple-element.430), channel_id=1, source_target_pairs={{0,4},{4,0},{1,5},{5,1},{2,6},{6,2},{3,7},{7,3},{8,12},{12,8},{9,1... | collective-permute-start | bytes 6291464 | tf_op jit(solution)/shard_map/ppermute | solution.py:619
  549.5 71.0 %collective-permute-start.59 = (bf16[256,2048]{1,0:T(8,128)(2,1)}, bf16[256,2048]{1,0:T(8,128)(2,1)}, u32[]{:S(2)}, u32[]{:S(2)}) collective-permute-start(bf16[256,2048]{1,0:T(8,128)(2,1)} %get-tuple-element.359), channel_id=1, source_target_pairs={{0,2},{1,3},{2,0},{3,1},{4,6},{5,7},{6,4},{7,5},{8,10},{9,11},{10,... | collective-permute-start | bytes 3145736 | tf_op jit(solution)/shard_map/ppermute | solution.py:619
  550.3 72.9 %collective-permute-start.58 = (bf16[256,2048]{1,0:T(8,128)(2,1)}, bf16[256,2048]{1,0:T(8,128)(2,1)}, u32[]{:S(2)}, u32[]{:S(2)}) collective-permute-start(bf16[256,2048]{1,0:T(8,128)(2,1)} %get-tuple-element.357), channel_id=1, source_target_pairs={{0,2},{1,3},{2,0},{3,1},{4,6},{5,7},{6,4},{7,5},{8,10},{9,11},{10,... | collective-permute-start | bytes 3145736 | tf_op jit(solution)/shard_map/ppermute | solution.py:619
  551.7 74.1 %collective-permute-start.60 = (bf16[256,2048]{1,0:T(8,128)(2,1)}, bf16[256,2048]{1,0:T(8,128)(2,1)}, u32[]{:S(2)}, u32[]{:S(2)}) collective-permute-start(bf16[256,2048]{1,0:T(8,128)(2,1)} %add.402), channel_id=1, source_target_pairs={{0,8},{8,16},{16,24},{24,0},{1,9},{9,17},{17,25},{25,1},{2,10},{10... | collective-permute-start | bytes 3145736 | tf_op jit(solution)/shard_map/ppermute | solution.py:624
  596.2 206.3 %reduce-scatter.3.cloned.1.call-start = ((), (), s32[]{:S(2)}) async-start(), calls=%async_computation.6 | async-start | bytes 9437184 | tf_op jit(solution)/shard_map/reduce_scatter | solution.py:950
  632.9 302.5 %reduce-scatter.5.cloned.1.call-start = ((), (), s32[]{:S(2)}) async-start(), calls=%async_computation.7 | async-start | bytes 7077888 | tf_op jit(solution)/shard_map/reduce_scatter | solution.py:1065
  637.8 69.6 %collective-permute-start.62 = (bf16[4,256,1024]{2,1,0:T(8,128)(2,1)}, bf16[4,256,1024]{2,1,0:T(8,128)(2,1)}, u32[]{:S(2)}, u32[]{:S(2)}) collective-permute-start(bf16[4,256,1024]{2,1,0:T(8,128)(2,1)} %get-tuple-element.428), channel_id=1, source_target_pairs={{0,4},{4,0},{1,5},{5,1},{2,6},{6,2},{3,7},{7,3},{8,12},{12,8},{9,1... | collective-permute-start | bytes 6291464 | tf_op jit(solution)/shard_map/ppermute | solution.py:619
  641.7 109.5 %collective-permute-start.64 = (bf16[256,1024]{1,0:T(8,128)(2,1)}, bf16[256,1024]{1,0:T(8,128)(2,1)}, u32[]{:S(2)}, u32[]{:S(2)}) collective-permute-start(bf16[256,1024]{1,0:T(8,128)(2,1)} %get-tuple-element.441), channel_id=1, source_target_pairs={{0,8},{8,16},{16,24},{24,0},{1,9},{9,17},{17,25},{25,1},{2,10},{10... | collective-permute-start | bytes 1572872 | tf_op jit(solution)/shard_map/ppermute | solution.py:624
  644.0 109.9 %collective-permute-start.65 = (bf16[256,1024]{1,0:T(8,128)(2,1)}, bf16[256,1024]{1,0:T(8,128)(2,1)}, u32[]{:S(2)}, u32[]{:S(2)}) collective-permute-start(bf16[256,1024]{1,0:T(8,128)(2,1)} %get-tuple-element.440), channel_id=1, source_target_pairs={{0,16},{8,24},{16,0},{24,8},{1,17},{9,25},{17,1},{25,9},{2,18},{10... | collective-permute-start | bytes 1572872 | tf_op jit(solution)/shard_map/ppermute | solution.py:624
  646.1 107.9 %collective-permute-start.66 = (bf16[256,1024]{1,0:T(8,128)(2,1)}, bf16[256,1024]{1,0:T(8,128)(2,1)}, u32[]{:S(2)}, u32[]{:S(2)}) collective-permute-start(bf16[256,1024]{1,0:T(8,128)(2,1)} %get-tuple-element.439), channel_id=1, source_target_pairs={{0,24},{8,0},{16,8},{24,16},{1,25},{9,1},{17,9},{25,17},{2,26},{10... | collective-permute-start | bytes 1572872 | tf_op jit(solution)/shard_map/ppermute | solution.py:624
  650.2 58.8 %collective-permute-start.61 = (bf16[256,2048]{1,0:T(8,128)(2,1)}, bf16[256,2048]{1,0:T(8,128)(2,1)}, u32[]{:S(2)}, u32[]{:S(2)}) collective-permute-start(bf16[256,2048]{1,0:T(8,128)(2,1)} %add.414), channel_id=1, source_target_pairs={{0,8},{8,16},{16,24},{24,0},{1,9},{9,17},{17,25},{25,1},{2,10},{10... | collective-permute-start | bytes 3145736 | tf_op jit(solution)/shard_map/ppermute | solution.py:624
  707.3 50.8 %collective-permute-start.71 = (bf16[256,2048]{1,0:T(8,128)(2,1)}, bf16[256,2048]{1,0:T(8,128)(2,1)}, u32[]{:S(2)}, u32[]{:S(2)}) collective-permute-start(bf16[256,2048]{1,0:T(8,128)(2,1)} %get-tuple-element.381), channel_id=1, source_target_pairs={{0,2},{1,3},{2,0},{3,1},{4,6},{5,7},{6,4},{7,5},{8,10},{9,11},{10,... | collective-permute-start | bytes 3145736 | tf_op jit(solution)/shard_map/ppermute | solution.py:619
  709.1 93.4 %collective-permute-start.70 = (bf16[4,128,2048]{2,1,0:T(8,128)(2,1)}, bf16[4,128,2048]{2,1,0:T(8,128)(2,1)}, u32[]{:S(2)}, u32[]{:S(2)}) collective-permute-start(bf16[4,128,2048]{2,1,0:T(8,128)(2,1)} %get-tuple-element.426), channel_id=1, source_target_pairs={{0,4},{4,0},{1,5},{5,1},{2,6},{6,2},{3,7},{7,3},{8,12},{12,8},{9,1... | collective-permute-start | bytes 6291464 | tf_op jit(solution)/shard_map/ppermute | solution.py:619
  751.2 51.3 %collective-permute-start.63 = (bf16[256,2048]{1,0:T(8,128)(2,1)}, bf16[256,2048]{1,0:T(8,128)(2,1)}, u32[]{:S(2)}, u32[]{:S(2)}) collective-permute-start(bf16[256,2048]{1,0:T(8,128)(2,1)} %add.417), channel_id=1, source_target_pairs={{0,8},{8,16},{16,24},{24,0},{1,9},{9,17},{17,25},{25,1},{2,10},{10... | collective-permute-start | bytes 3145736 | tf_op jit(solution)/shard_map/ppermute | solution.py:624
  754.0 48.5 %collective-permute-start.68 = (bf16[256,1024]{1,0:T(8,128)(2,1)S(1)}, bf16[256,1024]{1,0:T(8,128)(2,1)}, u32[]{:S(2)}, u32[]{:S(2)}) collective-permute-start(bf16[256,1024]{1,0:T(8,128)(2,1)S(1)} %get-tuple-element.436), channel_id=1, source_target_pairs={{0,16},{8,24},{16,0},{24,8},{1,17},{9,25},{17,1},{25,9},{2,18},{10... | collective-permute-start | bytes 1572872 | tf_op jit(solution)/shard_map/ppermute | solution.py:624
  758.2 44.3 %collective-permute-start.69 = (bf16[256,1024]{1,0:T(8,128)(2,1)S(1)}, bf16[256,1024]{1,0:T(8,128)(2,1)}, u32[]{:S(2)}, u32[]{:S(2)}) collective-permute-start(bf16[256,1024]{1,0:T(8,128)(2,1)S(1)} %get-tuple-element.435), channel_id=1, source_target_pairs={{0,24},{8,0},{16,8},{24,16},{1,25},{9,1},{17,9},{25,17},{2,26},{10... | collective-permute-start | bytes 1572872 | tf_op jit(solution)/shard_map/ppermute | solution.py:624
  846.4 73.4 %collective-permute-start.78 = (bf16[64,2048]{1,0:T(8,128)(2,1)S(1)}, bf16[64,2048]{1,0:T(8,128)(2,1)}, u32[]{:S(2)}, u32[]{:S(2)}) collective-permute-start(bf16[64,2048]{1,0:T(8,128)(2,1)S(1)} %get-tuple-element.451), channel_id=1, source_target_pairs={{0,8},{8,16},{16,24},{24,0},{1,9},{9,17},{17,25},{25,1},{2,10},{10... | collective-permute-start | bytes 786440 | tf_op jit(solution)/shard_map/ppermute | solution.py:624
  846.5 73.4 %collective-permute-start.79 = (bf16[64,2048]{1,0:T(8,128)(2,1)S(1)}, bf16[64,2048]{1,0:T(8,128)(2,1)}, u32[]{:S(2)}, u32[]{:S(2)}) collective-permute-start(bf16[64,2048]{1,0:T(8,128)(2,1)S(1)} %get-tuple-element.453), channel_id=1, source_target_pairs={{0,16},{8,24},{16,0},{24,8},{1,17},{9,25},{17,1},{25,9},{2,18},{10... | collective-permute-start | bytes 786440 | tf_op jit(solution)/shard_map/ppermute | solution.py:624
  847.1 72.7 %collective-permute-start.80 = (bf16[64,2048]{1,0:T(8,128)(2,1)S(1)}, bf16[64,2048]{1,0:T(8,128)(2,1)}, u32[]{:S(2)}, u32[]{:S(2)}) collective-permute-start(bf16[64,2048]{1,0:T(8,128)(2,1)S(1)} %get-tuple-element.452), channel_id=1, source_target_pairs={{0,24},{8,0},{16,8},{24,16},{1,25},{9,1},{17,9},{25,17},{2,26},{10... | collective-permute-start | bytes 786440 | tf_op jit(solution)/shard_map/ppermute | solution.py:624
  874.0 45.9 %collective-permute-start.77 = (f32[4,10,128]{2,1,0:T(8,128)S(1)}, f32[4,10,128]{2,1,0:T(8,128)S(1)}, u32[]{:S(2)}, u32[]{:S(2)}) collective-permute-start(f32[4,10,128]{2,1,0:T(8,128)S(1)} %dynamic-slice_bitcast_fusion.19), channel_id=1, source_target_pairs={{0,1},{1,0},{2,3},{3,2},{4,5},{5,4},{6,7},{7,6},{8,9},{9,8},{10,11... | collective-permute-start | bytes 61448 | tf_op jit(solution)/shard_map/ppermute | solution.py:619
  (158 other events, 3392.6 us)
Sparse Core Ops, SparseCore 0:
  12.0 83.5 all-gather.1
  633.0 105.4 reduce-scatter.2
  814.1 71.2 reduce-scatter.4
